TPU v7x, 32 devices: a whole 2x2x4 slice. The times are simulated.
32 devices in a mesh: section: 2 (over x), row: 2 (over y), col: 8 (over z, core).
Axes of the slice: x: 2, y: 2, z: 4, core: 2. Of those that a mesh axis runs over, the one named last changes fastest.
Arguments:
- images: bfloat16 [2, 2, 48, 32, 256], P('section', None, None, 'row', 'col'), may hold values from -6 to 6
- stem_first: bfloat16 [48, 256], replicated, may hold values from -0.875 to 0.875
- stem_conv: bfloat16 [3, 3, 256, 256], replicated, may hold values from -0.125 to 0.125
- patch_weight: bfloat16 [4096, 1024], P('col'), may hold values from -0.09375 to 0.09375
- position: bfloat16 [64, 8, 1024], P('col', 'row'), may hold values from -6 to 6
- gain_attn: float32 [1024], replicated, may hold values from 0.1 to 1.9
- w_qkv: bfloat16 [3, 1024, 1024], P(None, None, 'col'), may hold values from -0.5 to 0.5
- w_out: bfloat16 [1024, 1024], P('col'), may hold values from -0.1875 to 0.1875
- gain_mlp: float32 [1024], replicated, may hold values from 0.1 to 1.9
- w_up: bfloat16 [1024, 4096], P(None, 'col'), may hold values from -0.1875 to 0.1875
- w_down: bfloat16 [4096, 1024], P('col'), may hold values from -0.09375 to 0.09375
Outputs:
- encoded: bfloat16 [2, 2, 64, 8, 1024], P('section', 'row', 'col')
All inputs are finite; a program needn't handle non-finite values.
Results may differ from a plain program's by a relative error of at most 0.024.
The roundings to bfloat16 on the way count: a program that leaves them out, or rounds other values in their place, can miss the bound.
Values may be sent and summed in bfloat16 or wider, within the bound.
A program may use at most 64 MiB of HBM per device.

v0:
```python
import math

import jax
import jax.numpy as jnp
from jax import lax
from jax.sharding import PartitionSpec as P

HD = 64


def with_halo(block, sides, width):
    for axis, dim in sides:
        count = lax.axis_size(axis)
        forward = [(i, i + 1) for i in range(count - 1)]
        backward = [(target, source) for source, target in forward]
        low = lax.ppermute(
            lax.slice_in_dim(block, block.shape[dim] - width, None, axis=dim), axis, forward
        )
        high = lax.ppermute(lax.slice_in_dim(block, 0, width, axis=dim), axis, backward)
        block = jnp.concatenate([low, block, high], axis=dim)
    return block


def passed_along(value, axis, steps):
    count = lax.axis_size(axis)
    pairs = [(source, (source + steps) % count) for source in range(count)]
    return lax.ppermute(value, axis, pairs)


def layer_norm(vectors, gain_vec):
    row_mean = jnp.mean(vectors, axis=-1, keepdims=True)
    center = vectors - row_mean
    spread = jnp.mean(center * center, axis=-1, keepdims=True)
    return center * lax.rsqrt(spread + 1e-06) * gain_vec


def stem_features(images, stem_first, stem_conv):
    pixels = images[0]
    first_map = jnp.einsum("ikhw,kc->ihwc", pixels, stem_first, preferred_element_type=jnp.float32)
    stem_maps = jnp.maximum(first_map, 0.0).astype(jnp.bfloat16)
    padded = with_halo(stem_maps, (("row", 1), ("col", 2)), 1)
    img_count, height, tile_width, channels = stem_maps.shape
    summed = stem_maps.astype(jnp.float32)
    for offset_a in range(3):
        for offset_b in range(3):
            window = padded[:, offset_a : offset_a + height, offset_b : offset_b + tile_width, :]
            summed = summed + jnp.einsum(
                "ihwc,cd->ihwd",
                window,
                stem_conv[offset_a, offset_b],
                preferred_element_type=jnp.float32,
            )
    deep_maps = jnp.maximum(summed, 0.0).astype(jnp.bfloat16)
    blocks = deep_maps.reshape(img_count, height // 4, 4, tile_width // 4, 4, channels).transpose(
        0, 3, 1, 2, 4, 5
    )
    return blocks.reshape(img_count, tile_width // 4, height // 4, 16 * channels)


def on_device(
    images,
    stem_first,
    stem_conv,
    patch_weight,
    position,
    gain_attn,
    w_qkv,
    w_out,
    gain_mlp,
    w_up,
    w_down,
):
    features = stem_features(images, stem_first, stem_conv)
    img_count, cols_here, rows_here, feat_width = features.shape
    model_width = patch_weight.shape[1]
    flat_local = features.reshape(-1, feat_width)
    embedded = jnp.dot(
        flat_local,
        lax.all_gather(patch_weight, "col", axis=0, tiled=True),
        preferred_element_type=jnp.float32,
    )
    local_tokens = (
        embedded.reshape(img_count, cols_here, rows_here, model_width)
        + position.astype(jnp.float32)[None]
    ).astype(jnp.bfloat16)
    arrived = passed_along(local_tokens, "section", 1)
    token_image = lax.all_to_all(arrived, "row", split_axis=0, concat_axis=2, tiled=True)
    tokens_in = token_image.reshape(-1, model_width)
    residual = tokens_in.astype(jnp.float32)
    normed = layer_norm(residual, gain_attn).astype(jnp.bfloat16)
    projected = jnp.einsum(
        "td,kdh->kth",
        lax.all_gather(normed, "col", axis=0, tiled=True),
        w_qkv,
        preferred_element_type=jnp.float32,
    ).astype(jnp.bfloat16)
    token_count = projected.shape[1]
    local_heads = w_out.shape[0] // HD
    split_heads = projected.reshape(3, token_count, local_heads, HD).transpose(0, 2, 1, 3)
    key_heads = split_heads[1]
    value_heads = split_heads[2]
    block_rows = math.gcd(token_count, 512)
    query_blocks = (
        split_heads[0]
        .reshape(local_heads, token_count // block_rows, block_rows, HD)
        .transpose(1, 0, 2, 3)
    )

    def attend(query_block):
        scores = jnp.einsum(
            "hqd,hkd->hqk", query_block, key_heads, preferred_element_type=jnp.float32
        ) * HD ** (-0.5)
        row_peak = jnp.max(scores, axis=-1, keepdims=True)
        expo = jnp.exp(scores - row_peak)
        prob_rows = (expo / jnp.sum(expo, axis=-1, keepdims=True)).astype(jnp.bfloat16)
        return jnp.einsum(
            "hqk,hkd->hqd", prob_rows, value_heads, preferred_element_type=jnp.float32
        ).astype(jnp.bfloat16)

    attended = lax.map(attend, query_blocks)
    mixed_heads = attended.transpose(0, 2, 1, 3).reshape(token_count, local_heads * HD)
    row_slice = mixed_heads
    after = residual + lax.psum_scatter(
        jnp.dot(row_slice, w_out, preferred_element_type=jnp.float32).astype(jnp.bfloat16),
        "col",
        scatter_dimension=0,
        tiled=True,
    ).astype(jnp.float32)
    normed_mlp = layer_norm(after, gain_mlp).astype(jnp.bfloat16)
    hidden = jax.nn.gelu(
        jnp.dot(
            lax.all_gather(normed_mlp, "col", axis=0, tiled=True),
            w_up,
            preferred_element_type=jnp.float32,
        ),
        approximate=True,
    ).astype(jnp.bfloat16)
    row_slice = hidden
    encoded = (
        after
        + lax.psum_scatter(
            jnp.dot(row_slice, w_down, preferred_element_type=jnp.float32).astype(jnp.bfloat16),
            "col",
            scatter_dimension=0,
            tiled=True,
        ).astype(jnp.float32)
    ).astype(jnp.bfloat16)
    return encoded.reshape(1, 1, cols_here, -1, model_width)


def solution(mesh):
    placed = (
        P("section", None, None, "row", "col"),
        P(),
        P(),
        P("col", None),
        P("col", "row", None),
        P(),
        P(None, None, "col"),
        P("col", None),
        P(),
        P(None, "col"),
        P("col", None),
    )
    return jax.shard_map(
        on_device,
        mesh=mesh,
        in_specs=placed,
        out_specs=P("section", "row", "col", None, None),
        check_vma=False,
    )
```

profile of v0, /device:TPU:0, one launch (start us, length us, event | category | flops | bytes accessed | tf_op | source)
XLA Modules:
  0.0 239.8 jit_solution(17624231960715678657)
XLA Ops:
  6.5 0.7 all-gather.4.cloned.1.call-update
  7.3 1.2 fusion.12
  8.6 4.9 %collective-permute-start = (bf16[2,1,32,256]{3,2,1,0:T(8,128)(2,1)S(1)}, bf16[2,1,32,256]{3,2,1,0:T(8,128)(2,1)S(1)}, u32[]{:S(2)}, u32[]{:S(2)}) collective-permute-start(bf16[2,1,32,256]{3,2,1,0:T(8,128)(2,1)S(1)} %get-tuple-element.24), channel_id=1, source_target_pairs={{0,8},{1,9},{2,10},{3,11},{4,12},{5,13},{6,14},{7,15},{16,24},{17,... | collective-permute-start | bytes 98312 | tf_op jit(solution)/shard_map/ppermute | solution.py:16
  13.5 1.3 collective-permute-start.1
  15.1 4.2 %collective-permute-done.1 = bf16[2,1,32,256]{3,2,1,0:T(8,128)(2,1)S(1)} collective-permute-done((bf16[2,1,32,256]{3,2,1,0:T(8,128)(2,1)S(1)}, bf16[2,1,32,256]{3,2,1,0:T(8,128)(2,1)S(1)}, u32[]{:S(2)}, u32[]{:S(2)}) %collective-permute-start.1) | collective-permute-done | bytes 32800 | tf_op jit(solution)/shard_map/ppermute | solution.py:19
  19.3 1.3 collective-permute-start.2
  20.6 1.3 collective-permute-start.3
  22.6 3.0 %collective-permute-done.3 = bf16[2,18,1,256]{3,2,1,0:T(2,128)(2,1)S(1)} collective-permute-done((bf16[2,18,1,256]{3,2,1,0:T(2,128)(2,1)S(1)}, bf16[2,18,1,256]{3,2,1,0:T(2,128)(2,1)S(1)}, u32[]{:S(2)}, u32[]{:S(2)}) %collective-permute-start.3) | collective-permute-done | bytes 18464 | tf_op jit(solution)/shard_map/ppermute | solution.py:19
  25.6 0.5 maximum_maximum_fusion
  26.0 0.3 fusion.45
  26.4 0.3 fusion.38
  27.3 0.4 fusion.11
  27.7 0.4 fusion.13
  28.4 65.8 %all-gather.4.cloned.1.call-done = bf16[4096,1024]{1,0:T(8,128)(2,1)} async-done(((bf16[512,1024]{1,0:T(8,128)(2,1)}), bf16[4096,1024]{1,0:T(8,128)(2,1)}) %all-gather.4.cloned.1.call-update) | async-done | bytes 8388624 | tf_op jit(solution)/shard_map/all_gather | solution.py:79
  94.1 4.9 %fusion.17 = bf16[2,8,4,1024]{3,1,2,0:T(8,128)(2,1)S(1)} fusion(bf16[2,8,4,4096]{3,1,2,0:T(8,128)(2,1)S(1)} %bitcast.149, bf16[4096,1024]{1,0:T(8,128)(2,1)} %all-gather.4.cloned.1.call-done, f32[8,4,1024]{2,0,1:T(8,128)S(1)} %copy.24), kind=kOutput, calls=%fused_computation.25 | convolution fusion | flops 537001984 | bytes 9175040 | tf_op jit(solution)/shard_map/dot_general | solution.py:77
  99.1 1.5 collective-permute-start.4
  100.6 4.2 %collective-permute-done.4 = bf16[2,8,4,1024]{3,1,2,0:T(8,128)(2,1)S(1)} collective-permute-done((bf16[2,8,4,1024]{3,1,2,0:T(8,128)(2,1)S(1)}, bf16[2,8,4,1024]{3,1,2,0:T(8,128)(2,1)S(1)}, u32[]{:S(2)}, u32[]{:S(2)}) %collective-permute-start.4) | collective-permute-done | bytes 131104 | tf_op jit(solution)/shard_map/ppermute | solution.py:27
  104.8 7.0 %all_to_all.4 = bf16[2,8,4,1024]{3,1,2,0:T(8,128)(2,1)S(1)} all-to-all(bf16[2,8,4,1024]{3,1,2,0:T(8,128)(2,1)S(1)} %collective-permute-done.4), channel_id=1, replica_groups=mesh['section'=2,'row'=2,'col'=8] {'row'}, dimensions={0} | all-to-all | bytes 262144 | tf_op jit(solution)/shard_map/all_to_all | solution.py:87
  112.8 0.8 multiply_convert_fusion.1
  113.9 19.7 %all-gather.6.cloned.1.call-done = bf16[512,1024]{1,0:T(8,128)(2,1)} async-done(((bf16[64,1024]{1,0:T(8,128)(2,1)}), bf16[512,1024]{1,0:T(8,128)(2,1)}) %all-gather.6.cloned.1.call-update) | async-done | bytes 1048592 | tf_op jit(solution)/shard_map/all_gather | solution.py:93
  133.6 1.8 fusion.97
  135.5 0.8 fusion.94
  136.3 1.1 convolution_convert_fusion.2
  137.5 1.4 convolution_convert_fusion
  139.0 32.3 %reduce-scatter.3.cloned.1.call-done = bf16[64,1024]{1,0:T(8,128)(2,1)} async-done(((bf16[512,1024]{1,0:T(8,128)(2,1)}), bf16[64,1024]{1,0:T(8,128)(2,1)}) %reduce-scatter.3.cloned.1.call-update) | async-done | bytes 131088 | tf_op jit(solution)/shard_map/reduce_scatter | solution.py:123
  171.3 1.0 fusion.82
  172.3 1.1 multiply_reduce_fusion.1
  173.5 1.7 multiply_convert_fusion
  175.2 20.5 %all-gather.8.cloned.1.call-done = bf16[512,1024]{1,0:T(8,128)(2,1)} async-done(((bf16[64,1024]{1,0:T(8,128)(2,1)}), bf16[512,1024]{1,0:T(8,128)(2,1)}) %all-gather.8.cloned.1.call-update) | async-done | bytes 1048592 | tf_op jit(solution)/shard_map/all_gather | solution.py:132
  195.7 3.6 %convolution_convert_fusion.1 = bf16[512,1024]{1,0:T(8,128)(2,1)} fusion(bf16[512,1024]{1,0:T(8,128)(2,1)S(1)} %copy-done, bf16[512,1024]{1,0:T(8,128)(2,1)} %all-gather.8.cloned.1.call-done, bf16[1024,512]{1,0:T(8,128)(2,1)S(1)} %copy-done.8), kind=kOutput, calls=%fused_computation.9 | convolution fusion | flops 1076625408 | bytes 4194304 | tf_op jit(solution)/shard_map/dot_general | solution.py:142
  199.3 32.3 %reduce-scatter.5.cloned.1.call-done = bf16[64,1024]{1,0:T(8,128)(2,1)} async-done(((bf16[512,1024]{1,0:T(8,128)(2,1)}), bf16[64,1024]{1,0:T(8,128)(2,1)}) %reduce-scatter.5.cloned.1.call-update) | async-done | bytes 131088 | tf_op jit(solution)/shard_map/reduce_scatter | solution.py:141
  231.7 1.6 fusion.55
  (54 shorter events, 3.4 us)
Async XLA Ops:
  6.5 189.2 %copy-start = (bf16[512,1024]{1,0:T(8,128)(2,1)S(1)}, bf16[512,1024]{1,0:T(8,128)(2,1)}, u32[]{:S(2)}) copy-start(bf16[512,1024]{1,0:T(8,128)(2,1)} %param.21) | copy-start | bytes 3145732
  6.5 8.2 %copy-start.2 = (bf16[3,3,256,256]{3,2,1,0:T(8,128)(2,1)S(1)}, bf16[3,3,256,256]{3,2,1,0:T(8,128)(2,1)}, u32[]{:S(2)}) copy-start(bf16[3,3,256,256]{3,2,1,0:T(8,128)(2,1)} %param.13) | copy-start | bytes 3538948
  6.5 87.6 %all-gather.4.cloned.1.call-start = ((), (), s32[]{:S(2)}) async-start(), calls=%async_computation.3 | async-start | bytes 9437184 | tf_op jit(solution)/shard_map/all_gather | solution.py:79
  7.3 7.8 %copy-start.5 = (bf16[8,4,1024]{2,1,0:T(4,128)(2,1)S(1)}, bf16[8,4,1024]{2,1,0:T(4,128)(2,1)}, u32[]{:S(2)}) copy-start(bf16[8,4,1024]{2,1,0:T(4,128)(2,1)} %param.15) | copy-start | bytes 196612
  7.3 126.3 %all-gather.6.cloned.1.call-start = ((), (), s32[]{:S(2)}) async-start(), calls=%async_computation.4 | async-start | bytes 1179648 | tf_op jit(solution)/shard_map/all_gather | solution.py:93
  8.6 6.6 %collective-permute-start = (bf16[2,1,32,256]{3,2,1,0:T(8,128)(2,1)S(1)}, bf16[2,1,32,256]{3,2,1,0:T(8,128)(2,1)S(1)}, u32[]{:S(2)}, u32[]{:S(2)}) collective-permute-start(bf16[2,1,32,256]{3,2,1,0:T(8,128)(2,1)S(1)} %get-tuple-element.24), channel_id=1, source_target_pairs={{0,8},{1,9},{2,10},{3,11},{4,12},{5,13},{6,14},{7,15},{16,24},{17,... | collective-permute-start | bytes 98312 | tf_op jit(solution)/shard_map/ppermute | solution.py:16
  13.5 5.8 %collective-permute-start.1 = (bf16[2,1,32,256]{3,2,1,0:T(8,128)(2,1)S(1)}, bf16[2,1,32,256]{3,2,1,0:T(8,128)(2,1)S(1)}, u32[]{:S(2)}, u32[]{:S(2)}) collective-permute-start(bf16[2,1,32,256]{3,2,1,0:T(8,128)(2,1)S(1)} %get-tuple-element.25), channel_id=1, source_target_pairs={{8,0},{9,1},{10,2},{11,3},{12,4},{13,5},{14,6},{15,7},{24,16},{25,... | collective-permute-start | bytes 98312 | tf_op jit(solution)/shard_map/ppermute | solution.py:19
  19.3 3.2 %collective-permute-start.2 = (bf16[2,18,1,256]{3,2,1,0:T(2,128)(2,1)S(1)}, bf16[2,18,1,256]{3,2,1,0:T(2,128)(2,1)S(1)}, u32[]{:S(2)}, u32[]{:S(2)}) collective-permute-start(bf16[2,18,1,256]{3,2,1,0:T(2,128)(2,1)S(1)} %get-tuple-element.20), channel_id=1, source_target_pairs={{0,1},{1,2},{2,3},{3,4},{4,5},{5,6},{6,7},{8,9},{9,10},{10,11},{11... | collective-permute-start | bytes 55304 | tf_op jit(solution)/shard_map/ppermute | solution.py:16
  20.6 4.9 %collective-permute-start.3 = (bf16[2,18,1,256]{3,2,1,0:T(2,128)(2,1)S(1)}, bf16[2,18,1,256]{3,2,1,0:T(2,128)(2,1)S(1)}, u32[]{:S(2)}, u32[]{:S(2)}) collective-permute-start(bf16[2,18,1,256]{3,2,1,0:T(2,128)(2,1)S(1)} %get-tuple-element.22), channel_id=1, source_target_pairs={{1,0},{2,1},{3,2},{4,3},{5,4},{6,5},{7,6},{9,8},{10,9},{11,10},{12... | collective-permute-start | bytes 55304 | tf_op jit(solution)/shard_map/ppermute | solution.py:19
  99.1 13.7 %copy-start.6 = (f32[1024]{0:T(1024)S(1)}, f32[1024]{0:T(1024)}, u32[]{:S(2)}) copy-start(f32[1024]{0:T(1024)} %param.16) | copy-start | bytes 12292
  99.1 14.5 %copy-start.3 = (bf16[3,1024,128]{2,1,0:T(8,128)(2,1)S(1)}, bf16[3,1024,128]{2,1,0:T(8,128)(2,1)}, u32[]{:S(2)}) copy-start(bf16[3,1024,128]{2,1,0:T(8,128)(2,1)} %param.17) | copy-start | bytes 2359300
  99.1 5.7 %collective-permute-start.4 = (bf16[2,8,4,1024]{3,1,2,0:T(8,128)(2,1)S(1)}, bf16[2,8,4,1024]{3,1,2,0:T(8,128)(2,1)S(1)}, u32[]{:S(2)}, u32[]{:S(2)}) collective-permute-start(bf16[2,8,4,1024]{3,1,2,0:T(8,128)(2,1)S(1)} %fusion.17), channel_id=1, source_target_pairs={{0,16},{16,0},{1,17},{17,1},{2,18},{18,2},{3,19},{19,3},{4,20},{20... | collective-permute-start | bytes 393224 | tf_op jit(solution)/shard_map/ppermute | solution.py:27
  113.6 57.7 %reduce-scatter.3.cloned.1.call-start = ((), (), s32[]{:S(2)}) async-start(), calls=%async_computation.5 | async-start | bytes 1179648 | tf_op jit(solution)/shard_map/reduce_scatter | solution.py:123
  136.3 1.1 copy-start.4
  137.4 36.0 %copy-start.7 = (f32[1024]{0:T(1024)S(1)}, f32[1024]{0:T(1024)}, u32[]{:S(2)}) copy-start(f32[1024]{0:T(1024)} %param.19) | copy-start | bytes 12292
  138.9 56.8 %copy-start.8 = (bf16[1024,512]{1,0:T(8,128)(2,1)S(1)}, bf16[1024,512]{1,0:T(8,128)(2,1)}, u32[]{:S(2)}) copy-start(bf16[1024,512]{1,0:T(8,128)(2,1)} %param.20) | copy-start | bytes 3145732
  138.9 56.8 %all-gather.8.cloned.1.call-start = ((), (), s32[]{:S(2)}) async-start(), calls=%async_computation.6 | async-start | bytes 1179648 | tf_op jit(solution)/shard_map/all_gather | solution.py:132
  175.1 56.5 %copy-start.1 = (bf16[64,1024]{1,0:T(8,128)(2,1)S(1)}, bf16[64,1024]{1,0:T(8,128)(2,1)}, u32[]{:S(2)}) copy-start(bf16[64,1024]{1,0:T(8,128)(2,1)} %reduce-scatter.3.cloned.1.call-done) | copy-start | bytes 393220
  175.2 56.5 %reduce-scatter.5.cloned.1.call-start = ((), (), s32[]{:S(2)}) async-start(), calls=%async_computation.7 | async-start | bytes 1179648 | tf_op jit(solution)/shard_map/reduce_scatter | solution.py:141
Sparse Core Ops, SparseCore 0:
  8.9 85.1 all-gather.3
  113.7 19.8 all-gather.5
  139.0 32.1 reduce-scatter.2
  175.3 20.4 all-gather.7
  199.5 32.1 reduce-scatter.4
where the time goes:
time: 240 us
  waiting for transfers between devices  183 us (76%)
  matrix products  17.9 us (7%)
  between operations  13.4 us (6%)
  starting transfers between devices  10.5 us (4%)
  other arithmetic  7.1 us (3%)
  blocking collectives  6.96 us (3%)
    all_gather x1, waiting for transfers between devices, on_device(): lax.all_gather(patch_weight, 'col', axis=0, tiled=True)  65.8 us
    reduce_scatter x1, waiting for transfers between devices, on_device(): lax.psum_scatter(jnp.dot(row_slice, w_down, preferred_element_type=jnp.fl...  32.3 us
    reduce_scatter x1, waiting for transfers between devices, on_device(): lax.psum_scatter(jnp.dot(row_slice, w_out, preferred_element_type=jnp.flo...  32.3 us
    all_gather x1, waiting for transfers between devices, on_device(): lax.all_gather(normed_mlp, 'col', axis=0, tiled=True)  20.5 us
    all_gather x1, waiting for transfers between devices, on_device(): lax.all_gather(normed, 'col', axis=0, tiled=True)  19.7 us
    ppermute x2, waiting for transfers between devices, with_halo(): lax.ppermute(lax.slice_in_dim(block, 0, width, axis=dim), axis, backward)  7.15 us
    all_to_all x1, blocking collectives, on_device(): lax.all_to_all(arrived, 'row', split_axis=0, concat_axis=2, tiled=True)  6.96 us
    ppermute x2, starting transfers between devices, with_halo(): lax.ppermute(lax.slice_in_dim(block, block.shape[dim] - width, None, axis...  6.2 us
  transfers between devices with their start and end apart: 10, of which 8 were waited for; matrix products, arithmetic and copies ran while one was open for 2% of the time, Pallas kernels for 0%

commit v1 on v0

--- a/solution.py
+++ b/solution.py
@@ -1,30 +1,224 @@
+import functools
 import math
 
 import jax
 import jax.numpy as jnp
 from jax import lax
+from jax.experimental import pallas as pl
+from jax.experimental.pallas import tpu as pltpu
 from jax.sharding import PartitionSpec as P
 
 HD = 64
-
-
-def with_halo(block, sides, width):
-    for axis, dim in sides:
-        count = lax.axis_size(axis)
-        forward = [(i, i + 1) for i in range(count - 1)]
-        backward = [(target, source) for source, target in forward]
-        low = lax.ppermute(
-            lax.slice_in_dim(block, block.shape[dim] - width, None, axis=dim), axis, forward
-        )
-        high = lax.ppermute(lax.slice_in_dim(block, 0, width, axis=dim), axis, backward)
-        block = jnp.concatenate([low, block, high], axis=dim)
-    return block
-
-
-def passed_along(value, axis, steps):
-    count = lax.axis_size(axis)
-    pairs = [(source, (source + steps) % count) for source in range(count)]
-    return lax.ppermute(value, axis, pairs)
+V = pltpu.VMEM
+
+
+def call(body, out, ins, scratch, cid, name, **kw):
+    return pl.pallas_call(body, out_shape=out,
+        in_specs=[pl.BlockSpec(memory_space=pltpu.VMEM)]*len(ins),
+        out_specs=jax.tree.map(lambda _: pl.BlockSpec(memory_space=pltpu.VMEM), out),
+        scratch_shapes=scratch, name=name,
+        compiler_params=pltpu.CompilerParams(collective_id=cid, has_side_effects=True, vmem_limit_bytes=48<<20))(*ins)
+
+
+def rc(src, dst, ss, rs, **dev):
+    return pltpu.make_async_remote_copy(src_ref=src, dst_ref=dst, send_sem=ss, recv_sem=rs, device_id=dev, device_id_type=pl.DeviceIdType.MESH)
+
+
+def greet(devs):
+    b = pltpu.get_barrier_semaphore()
+    for d in devs:
+        pl.semaphore_signal(b, inc=1, device_id=d, device_id_type=pl.DeviceIdType.MESH)
+    pl.semaphore_wait(b, len(devs))
+
+
+def ag_hier(x, cid):
+    n = lax.axis_size("col"); zs = n//2
+    def body(x_ref, o_ref, s1, s2, r1, r2, sp, rp, ls):
+        me = lax.axis_index("col"); z = me//2; p = lax.rem(me,2); mate = me+1-2*p
+        far = [lax.rem(me+2*k, n) for k in range(1, zs)]
+        greet([{"col": mate}]+[{"col": d} for d in far])
+        cs=[]
+        for k in range(1,zs):
+            c = rc(x_ref, o_ref.at[me], s1.at[k], r1.at[zs-k], col=far[k-1]); c.start(); cs.append(c)
+        c = rc(x_ref, o_ref.at[me], sp, rp, col=mate); c.start(); cs.append(c)
+        l = pltpu.make_async_copy(x_ref, o_ref.at[me], ls); l.start()
+        order = sorted(range(1,zs), key=lambda k: min(k, zs-k))
+        for k in order:
+            src = far[k-1]
+            rc(x_ref, o_ref.at[src], s1.at[k], r1.at[k], col=mate).wait_recv()
+            c = rc(o_ref.at[src], o_ref.at[src], s2.at[k], r2.at[k], col=mate); c.start(); cs.append(c)
+        l.wait()
+        rc(x_ref, o_ref.at[mate], sp, rp, col=mate).wait_recv()
+        for k in order:
+            src = lax.rem(mate+2*k, n)
+            rc(x_ref, o_ref.at[src], s2.at[k], r2.at[k], col=mate).wait_recv()
+        for c in cs: c.wait_send()
+    D=pltpu.SemaphoreType.DMA
+    return call(body, jax.ShapeDtypeStruct((n,)+x.shape, x.dtype), [x], [D((zs,)),D((zs,)),D((zs,)),D((zs,)),D,D,D], cid, "aghier%d"%cid)
+
+
+def rs_hier(parts, cid):
+    n = lax.axis_size("col"); zs = n//2
+    blk = parts.shape[1:]
+    def body(x_ref, o_ref, buf1, stage, buf2, s1, r1, s2, r2):
+        me = lax.axis_index("col"); z = me//2; p = lax.rem(me,2); mate = me+1-2*p
+        far = [lax.rem(me+2*k, n) for k in range(zs)]
+        matefar = [lax.rem(mate+2*k, n) for k in range(zs)]
+        greet([{"col": mate}]+[{"col": d} for d in far[1:]])
+        order = sorted(range(1,zs), key=lambda k: -min(k, zs-k)) + [0]
+        cs=[]
+        for k in order:
+            c = rc(x_ref.at[matefar[k]], buf1.at[k], s1.at[k], r1.at[k], col=mate); c.start(); cs.append(c)
+        for k in order:
+            rc(x_ref.at[0], buf1.at[k], s1.at[k], r1.at[k], col=mate).wait_recv()
+            tot = x_ref[far[k]].astype(jnp.float32) + buf1[k].astype(jnp.float32)
+            if k:
+                stage[k] = tot.astype(stage.dtype)
+                c = rc(stage.at[k], buf2.at[zs-k], s2.at[k], r2.at[zs-k], col=far[k]); c.start(); cs.append(c)
+        for k in order[::-1][1:]:
+            rc(stage.at[0], buf2.at[k], s2.at[k], r2.at[k], col=mate).wait_recv()
+            tot = tot + buf2[k].astype(jnp.float32)
+        o_ref[...] = tot
+        for c in cs: c.wait_send()
+    D=pltpu.SemaphoreType.DMA
+    return call(body, jax.ShapeDtypeStruct(blk, jnp.float32), [parts], [V((zs,)+blk, parts.dtype)]*3+[D((zs,)),D((zs,)),D((zs,)),D((zs,))], cid, "rshier%d"%cid)
+
+
+def a2a_col(x, cid):
+    n = lax.axis_size("col")
+
+    def body(x_ref, o_ref, ss, rs, ls):
+        me = lax.axis_index("col")
+        greet([{"col": lax.rem(me + k, n)} for k in range(1, n)])
+        cs = []
+        for k in range(1, n):
+            d = lax.rem(me + k, n)
+            c = rc(x_ref.at[d], o_ref.at[me], ss.at[k], rs.at[n - k], col=d)
+            c.start()
+            cs.append(c)
+        own = pltpu.make_async_copy(x_ref.at[me], o_ref.at[me], ls)
+        own.start()
+        own.wait()
+        for k in range(1, n):
+            d = lax.rem(me + k, n)
+            rc(x_ref.at[d], o_ref.at[d], ss.at[k], rs.at[k], col=d).wait_recv()
+        for c in cs:
+            c.wait_send()
+
+    D = pltpu.SemaphoreType.DMA
+    return call(
+        body, jax.ShapeDtypeStruct(x.shape, x.dtype), [x], [D((n,)), D((n,)), D], cid, "spread"
+    )
+
+
+def swap_groups(x, cid):
+    count = lax.axis_size("row")
+    secs = lax.axis_size("section")
+
+    def body(x_ref, o_ref, ss, rs):
+        s, r = lax.axis_index("section"), lax.axis_index("row")
+        to = lax.rem(s + 1, secs)
+        back = lax.rem(s + secs - 1, secs)
+        b = pltpu.get_barrier_semaphore()
+        for k in range(count):
+            pl.semaphore_signal(
+                b,
+                inc=1,
+                device_id={"section": back, "row": lax.rem(r + k, count)},
+                device_id_type=pl.DeviceIdType.MESH,
+            )
+        pl.semaphore_wait(b, count)
+        cs = []
+        for k in range(count):
+            d = lax.rem(r + k, count)
+            c = rc(x_ref.at[d], o_ref.at[r], ss.at[k], rs.at[(count - k) % count], section=to, row=d)
+            c.start()
+            cs.append(c)
+        for k in range(count):
+            d = lax.rem(r + k, count)
+            rc(x_ref.at[d], o_ref.at[d], ss.at[k], rs.at[k], section=to, row=d).wait_recv()
+        for c in cs:
+            c.wait_send()
+
+    D = pltpu.SemaphoreType.DMA
+    return call(
+        body, jax.ShapeDtypeStruct(x.shape, x.dtype), [x], [D((count,)), D((count,))], cid, "swap"
+    )
+
+
+def halo(first, cid):
+    imgs, height, width, ch = first.shape
+    rows_n, cols_n = lax.axis_size("row"), lax.axis_size("col")
+    steps = [(a, b) for a in (-1, 0, 1) for b in (-1, 0, 1) if (a, b) != (0, 0)]
+    edge = {-1: slice(0, 1), 0: slice(None), 1: slice(-1, None)}
+    ins = [first[:, edge[a], edge[b], :].reshape(-1, ch) for a, b in steps]
+
+    def body(*refs):
+        src, dst = refs[:8], refs[8:16]
+        ss, rs = refs[16:]
+        r, c = lax.axis_index("row"), lax.axis_index("col")
+        bar = pltpu.get_barrier_semaphore()
+
+        def there(a, b):
+            ok = jnp.int32(1)
+            if a == -1:
+                ok = ok * (r > 0).astype(jnp.int32)
+            if a == 1:
+                ok = ok * (r < rows_n - 1).astype(jnp.int32)
+            if b == -1:
+                ok = ok * (c > 0).astype(jnp.int32)
+            if b == 1:
+                ok = ok * (c < cols_n - 1).astype(jnp.int32)
+            return ok
+
+        have = [there(a, b) for a, b in steps]
+        total = functools.reduce(lambda p, q: p + q, have)
+        for (a, b), ok in zip(steps, have):
+
+            @pl.when(ok == 1)
+            def _():
+                pl.semaphore_signal(
+                    bar,
+                    inc=1,
+                    device_id={"row": r + a, "col": c + b},
+                    device_id_type=pl.DeviceIdType.MESH,
+                )
+
+        pl.semaphore_wait(bar, total)
+        for i, ((a, b), ok) in enumerate(zip(steps, have)):
+
+            @pl.when(ok == 1)
+            def _():
+                rc(src[i], dst[7 - i], ss.at[i], rs.at[7 - i], row=r + a, col=c + b).start()
+
+            @pl.when(ok == 0)
+            def _():
+                dst[i][...] = jnp.zeros_like(dst[i])
+
+        for i, ((a, b), ok) in enumerate(zip(steps, have)):
+
+            @pl.when(ok == 1)
+            def _():
+                desc = rc(src[i], dst[i], ss.at[i], rs.at[i], row=r + a, col=c + b)
+                desc.wait_recv()
+                desc.wait_send()
+
+    D = pltpu.SemaphoreType.DMA
+    outs = call(
+        body,
+        tuple(jax.ShapeDtypeStruct(v.shape, v.dtype) for v in ins),
+        ins,
+        [D((8,)), D((8,))],
+        cid,
+        "halo",
+    )
+    got = {}
+    for (a, b), v in zip(steps, outs):
+        got[a, b] = v.reshape(imgs, height if a == 0 else 1, width if b == 0 else 1, ch)
+    got[0, 0] = first
+    return jnp.concatenate(
+        [jnp.concatenate([got[a, b] for b in (-1, 0, 1)], axis=2) for a in (-1, 0, 1)], axis=1
+    )
 
 
 def layer_norm(vectors, gain_vec):
@@ -38,7 +232,7 @@
     pixels = images[0]
     first_map = jnp.einsum("ikhw,kc->ihwc", pixels, stem_first, preferred_element_type=jnp.float32)
     stem_maps = jnp.maximum(first_map, 0.0).astype(jnp.bfloat16)
-    padded = with_halo(stem_maps, (("row", 1), ("col", 2)), 1)
+    padded = halo(stem_maps, 0)
     img_count, height, tile_width, channels = stem_maps.shape
     summed = stem_maps.astype(jnp.float32)
     for offset_a in range(3):
@@ -74,23 +268,29 @@
     img_count, cols_here, rows_here, feat_width = features.shape
     model_width = patch_weight.shape[1]
     flat_local = features.reshape(-1, feat_width)
-    embedded = jnp.dot(
-        flat_local,
-        lax.all_gather(patch_weight, "col", axis=0, tiled=True),
-        preferred_element_type=jnp.float32,
-    )
+    n = lax.axis_size("col")
+    rows_n = lax.axis_size("row")
+    here = flat_local.shape[0]
+    pieces = a2a_col(flat_local.reshape(here, n, -1).transpose(1, 0, 2), 1)
+    terms = jnp.dot(
+        pieces.reshape(n * here, -1), patch_weight, preferred_element_type=jnp.float32
+    ).astype(jnp.bfloat16)
+    embedded = rs_hier(terms.reshape(n, here, model_width), 2)
     local_tokens = (
         embedded.reshape(img_count, cols_here, rows_here, model_width)
         + position.astype(jnp.float32)[None]
     ).astype(jnp.bfloat16)
-    arrived = passed_along(local_tokens, "section", 1)
-    token_image = lax.all_to_all(arrived, "row", split_axis=0, concat_axis=2, tiled=True)
-    tokens_in = token_image.reshape(-1, model_width)
+    arrived = swap_groups(local_tokens.reshape(rows_n, -1, model_width), 3)
+    tokens_in = (
+        arrived.reshape(rows_n, img_count // rows_n, cols_here, rows_here, model_width)
+        .transpose(1, 2, 0, 3, 4)
+        .reshape(-1, model_width)
+    )
     residual = tokens_in.astype(jnp.float32)
     normed = layer_norm(residual, gain_attn).astype(jnp.bfloat16)
     projected = jnp.einsum(
         "td,kdh->kth",
-        lax.all_gather(normed, "col", axis=0, tiled=True),
+        ag_hier(normed, 4).reshape(-1, model_width),
         w_qkv,
         preferred_element_type=jnp.float32,
     ).astype(jnp.bfloat16)
@@ -120,16 +320,16 @@
     attended = lax.map(attend, query_blocks)
     mixed_heads = attended.transpose(0, 2, 1, 3).reshape(token_count, local_heads * HD)
     row_slice = mixed_heads
-    after = residual + lax.psum_scatter(
-        jnp.dot(row_slice, w_out, preferred_element_type=jnp.float32).astype(jnp.bfloat16),
-        "col",
-        scatter_dimension=0,
-        tiled=True,
-    ).astype(jnp.float32)
+    after = residual + rs_hier(
+        jnp.dot(row_slice, w_out, preferred_element_type=jnp.float32)
+        .astype(jnp.bfloat16)
+        .reshape(n, -1, model_width),
+        5,
+    )
     normed_mlp = layer_norm(after, gain_mlp).astype(jnp.bfloat16)
     hidden = jax.nn.gelu(
         jnp.dot(
-            lax.all_gather(normed_mlp, "col", axis=0, tiled=True),
+            ag_hier(normed_mlp, 6).reshape(-1, model_width),
             w_up,
             preferred_element_type=jnp.float32,
         ),
@@ -138,12 +338,12 @@
     row_slice = hidden
     encoded = (
         after
-        + lax.psum_scatter(
-            jnp.dot(row_slice, w_down, preferred_element_type=jnp.float32).astype(jnp.bfloat16),
-            "col",
-            scatter_dimension=0,
-            tiled=True,
-        ).astype(jnp.float32)
+        + rs_hier(
+        jnp.dot(row_slice, w_down, preferred_element_type=jnp.float32)
+        .astype(jnp.bfloat16)
+        .reshape(n, -1, model_width),
+        7,
+    )
     ).astype(jnp.bfloat16)
     return encoded.reshape(1, 1, cols_here, -1, model_width)
 

time: 240 us -> 134 us (0.56)
  waiting for transfers between devices: 183 us -> 0 us
  Pallas kernels: 0 us -> 105 us
  between operations: 13.4 us -> 0.44 us
  starting transfers between devices: 10.5 us -> 0 us
  matrix products: 17.9 us -> 10.6 us
  blocking collectives: 6.96 us -> 0 us
  other arithmetic: 7.1 us -> 12.2 us
  local copies, waits for them, and re-layouts: 1.22 us -> 6.28 us
    all_gather x3 -> x0, waiting for transfers between devices: 106 us -> none  [the longest x1 65.8 us: on_device(): lax.all_gather(patch_weight, 'col', axis=0, tiled=True)]
    pallas_call x0 -> x8, Pallas kernels: none -> 105 us  [call(): pl.pallas_call(body, out_shape=out, in_specs=[pl.BlockSpec(memory_space=p...]
    reduce_scatter x2 -> x0, waiting for transfers between devices: 64.6 us -> none  [the longest x1 32.3 us: on_device(): lax.psum_scatter(jnp.dot(row_slice, w_down, preferred_element_type=jnp.fl...]
    ppermute x5 -> x0, waiting for transfers between devices: 11.3 us -> none  [the longest x2 7.15 us: with_halo(): lax.ppermute(lax.slice_in_dim(block, 0, width, axis=dim), axis, backward)]
    ppermute x5 -> x0, starting transfers between devices: 10.3 us -> none  [the longest x2 6.2 us: with_halo(): lax.ppermute(lax.slice_in_dim(block, block.shape[dim] - width, None, axis...]
    all_to_all x1 -> x0, blocking collectives: 6.96 us -> none  [on_device(): lax.all_to_all(arrived, 'row', split_axis=0, concat_axis=2, tiled=True)]
    convert_element_type x2 -> x4, other arithmetic: 0.07 us -> 6.94 us  [the longest x1 6.3 us: stem_features(): deep_maps = jnp.maximum(summed, 0.0).astype(jnp.bfloat16)]
    dot_general x1, matrix products: 4.95 us -> 0.71 us  [on_device(): jnp.dot(pieces.reshape(n * here, -1), patch_weight, preferred_element_typ...]
  transfers between devices with their start and end apart: 10 -> 0, of which waited for: 8 -> 0; matrix products, arithmetic and copies ran while one was open for 2% -> 0% of each run, Pallas kernels for 0% -> 0%
where the time goes in v1:
time: 134 us
  Pallas kernels  105 us (78%)
  other arithmetic  12.2 us (9%)
  matrix products  10.6 us (8%)
  local copies, waits for them, and re-layouts  6.28 us (5%)
    pallas_call x8, Pallas kernels, call(): pl.pallas_call(body, out_shape=out, in_specs=[pl.BlockSpec(memory_space=p...  105 us
    convert_element_type x1, other arithmetic, stem_features(): deep_maps = jnp.maximum(summed, 0.0).astype(jnp.bfloat16)  6.3 us
    slice x1, local copies, waits for them, and re-layouts, stem_features(): padded[:, offset_a:offset_a + height, offset_b:offset_b + tile_width, :]  3.5 us
    dot_general x1, matrix products, on_device(): jnp.dot(row_slice, w_down, preferred_element_type=jnp.float32)  2.92 us
    concatenate x1, other arithmetic, halo(): jnp.concatenate([jnp.concatenate([got[a, b] for b in (-1, 0, 1)], axis=2)...  2.91 us

profile of v1, /device:TPU:0, one launch (start us, length us, event | category | flops | bytes accessed | tf_op | source)
XLA Modules:
  0.0 134.2 jit_solution(14772517865786129048)
XLA Ops:
  0.0 1.3 fusion.37
  1.3 0.6 fusion.12
  2.0 5.8 %halo.1 = (bf16[2,256]{1,0:T(2,128)(2,1)S(1)}, bf16[64,256]{1,0:T(8,128)(2,1)S(1)}, bf16[2,256]{1,0:T(2,128)(2,1)S(1)}, bf16[32,256]{1,0:T(8,128)(2,1)S(1)}, bf1...) custom-call(bf16[2,256]{1,0:T(2,128)(2,1)S(1)} %get-tuple-element.51, ...), custom_call_target="tpu_custom_call" | custom-call | tf_op jit(solution)/shard_map/halo/pallas_call | solution.py:16
  8.0 2.9 %maximum_maximum_fusion = (bf16[2,17,34,256]{3,0,2,1:T(2,128)(2,1)S(1)}, bf16[2,17,34,256]{3,0,2,1:T(2,128)(2,1)S(1)}) fusion(bf16[2,16,1,256]{3,0,2,1:T(2,128)(2,1)S(1)} %copy.76, bf16[2,16,32,256]{3,0,2,1:T(2,128)(2,1)S(1)} %fusion.12, bf16[2,16,1,256]{3,0,2,1:T(2,128)(2,1)S(1)} %copy.75, bf16[2,1,1,256]{3,0,2,1:T(2,128)(2,1)S(1)} %bitcast.181, ...), kind=kLoop, calls=%fused_computation.32 | loop fusion | flops 2959360 | bytes 1810432 | tf_op jit(solution)/shard_map/concatenate | solution.py:219
  10.9 3.5 %fusion.76 = (bf16[2,16,32,256]{3,0,2,1:T(2,128)(2,1)S(1)}, bf16[2,16,32,256]{3,0,2,1:T(2,128)(2,1)S(1)}, bf16[2,16,32,256]{3,0,2,1:T(2,128)(2,1)S(1)}, bf16[2,1...) fusion(bf16[2,17,34,256]{3,0,2,1:T(2,128)(2,1)S(1)} %get-tuple-element.4, ...), kind=kLoop, calls=%fused_computation.111 | loop fusion | bytes 6291456 | tf_op jit(solution)/shard_map/slice | solution.py:240
  14.4 0.3 fusion.15
  14.7 0.3 fusion.17
  15.0 0.3 fusion.19
  15.3 0.3 fusion.27
  15.6 0.3 fusion.29
  15.9 0.3 fusion.31
  16.2 0.8 pad_maximum_fusion.1
  17.0 0.3 fusion.21
  17.3 0.3 fusion.25
  17.6 0.3 fusion.23
  17.9 6.3 %fusion.11 = bf16[2,16,32,256]{3,0,2,1:T(2,128)(2,1)S(1)} fusion(f32[2,16,32,256]{3,2,1,0:T(8,128)S(1)} %fusion.15, f32[2,16,32,256]{3,2,1,0:T(8,128)S(1)} %fusion.17, f32[2,16,32,256]{3,2,1,0:T(8,128)S(1)} %fusion.19, f32[2,16,32,256]{3,2,1,0:T(8,128)S(1)} %fusion.21, f32[2,16,32,256]{3,2,1,0:T(8,128)S(1)} %fusion.23, f32[2,16,32,256]{3,2,1,0:T(8,128)S(1)} %fusion.25, ...), kind=kLoop, calls=%fused_computation.20 | loop fusion | flops 3670016 | bytes 10485760 | tf_op jit(solution)/shard_map/convert_element_type | solution.py:247
  24.4 0.3 reshape_reshape_reshape.3
  24.9 12.8 %spread.1 = bf16[8,64,512]{2,1,0:T(8,128)(2,1)S(1)} custom-call(bf16[8,64,512]{2,1,0:T(8,128)(2,1)S(1)} %bitcast.166), custom_call_target="tpu_custom_call" | custom-call | tf_op jit(solution)/shard_map/spread/pallas_call | solution.py:16
  37.8 0.7 convolution_convert_fusion.2
  38.5 17.0 %rshier2.1 = f32[64,1024]{1,0:T(8,128)S(1)} custom-call(bf16[8,64,1024]{2,1,0:T(8,128)(2,1)S(1)} %bitcast.167), custom_call_target="tpu_custom_call" | custom-call | tf_op jit(solution)/shard_map/rshier2/pallas_call | solution.py:16
  55.6 6.2 %swap.1 = bf16[2,32,1024]{2,1,0:T(8,128)(2,1)S(1)} custom-call(bf16[2,32,1024]{2,1,0:T(8,128)(2,1)S(1)} %add_convert_fusion.1.x_ref), custom_call_target="tpu_custom_call" | custom-call | tf_op jit(solution)/shard_map/swap/pallas_call | solution.py:16
  62.7 14.9 %aghier4.1 = bf16[8,64,1024]{2,1,0:T(8,128)(2,1)S(1)} custom-call(bf16[64,1024]{1,0:T(8,128)(2,1)S(1)} %multiply_convert_fusion.1.x_ref), custom_call_target="tpu_custom_call" | custom-call | tf_op jit(solution)/shard_map/aghier4/pallas_call | solution.py:16
  77.6 1.4 %copy.102 = bf16[3,1024,128]{1,2,0:T(8,128)(2,1)S(1)} copy(bf16[3,1024,128]{2,1,0:T(8,128)(2,1)} %param.17) | data formatting | bytes 1572864 | tf_op args[6]
  79.0 0.6 fusion.83
  79.7 0.8 fusion.80
  80.6 1.1 convolution_convert_fusion.3
  81.7 0.4 convolution_convert_fusion
  82.2 16.4 %rshier5.1 = f32[64,1024]{1,0:T(8,128)S(1)} custom-call(bf16[8,64,1024]{2,1,0:T(8,128)(2,1)S(1)} %bitcast.164), custom_call_target="tpu_custom_call" | custom-call | tf_op jit(solution)/shard_map/rshier5/pallas_call | solution.py:16
  99.0 15.7 %aghier6.1 = bf16[8,64,1024]{2,1,0:T(8,128)(2,1)S(1)} custom-call(bf16[64,1024]{1,0:T(8,128)(2,1)S(1)} %multiply_convert_fusion.x_ref), custom_call_target="tpu_custom_call" | custom-call | tf_op jit(solution)/shard_map/aghier6/pallas_call | solution.py:16
  114.7 2.9 %convolution_convert_fusion.1 = bf16[512,1024]{1,0:T(8,128)(2,1)S(1)} fusion(bf16[512,1024]{1,0:T(8,128)(2,1)} %param.21, bf16[512,1024]{1,0:T(8,128)(2,1)S(1)} %bitcast.170, bf16[1024,512]{1,0:T(8,128)(2,1)} %param.20), kind=kOutput, calls=%fused_computation.7 | convolution fusion | flops 1076625408 | bytes 4194304 | tf_op jit(solution)/shard_map/dot_general | solution.py:342
  117.6 15.9 %rshier7.1 = f32[64,1024]{1,0:T(8,128)S(1)} custom-call(bf16[8,64,1024]{2,1,0:T(8,128)(2,1)S(1)} %bitcast.168), custom_call_target="tpu_custom_call" | custom-call | tf_op jit(solution)/shard_map/rshier7/pallas_call | solution.py:16
  133.5 0.7 fusion.41
  (43 shorter events, 2.0 us)
Async XLA Ops:
  0.0 37.8 %copy-start = (bf16[512,1024]{1,0:T(8,128)(2,1)S(1)}, bf16[512,1024]{1,0:T(8,128)(2,1)}, u32[]{:S(2)}) copy-start(bf16[512,1024]{1,0:T(8,128)(2,1)} %param.14) | copy-start | bytes 3145732
  10.9 3.5 %copy-start.1 = (bf16[3,3,256,256]{3,2,1,0:T(8,128)(2,1)S(1)}, bf16[3,3,256,256]{3,2,1,0:T(8,128)(2,1)}, u32[]{:S(2)}) copy-start(bf16[3,3,256,256]{3,2,1,0:T(8,128)(2,1)} %param.13) | copy-start | bytes 3538948
  38.5 17.0 %copy-start.3 = (bf16[8,4,1024]{2,1,0:T(4,128)(2,1)S(1)}, bf16[8,4,1024]{2,1,0:T(4,128)(2,1)}, u32[]{:S(2)}) copy-start(bf16[8,4,1024]{2,1,0:T(4,128)(2,1)} %param.15) | copy-start | bytes 196612
  55.6 7.0 %copy-start.4 = (f32[1024]{0:T(1024)S(1)}, f32[1024]{0:T(1024)}, u32[]{:S(2)}) copy-start(f32[1024]{0:T(1024)} %param.16) | copy-start | bytes 12292
  80.6 1.1 copy-start.2
  82.2 16.7 %copy-start.5 = (f32[1024]{0:T(1024)S(1)}, f32[1024]{0:T(1024)}, u32[]{:S(2)}) copy-start(f32[1024]{0:T(1024)} %param.19) | copy-start | bytes 12292

commit v2 on v1

v2 whole, which is shorter than its diff:
```python
import functools
import math

import jax
import jax.numpy as jnp
from jax import lax
from jax.experimental import pallas as pl
from jax.experimental.pallas import tpu as pltpu
from jax.sharding import PartitionSpec as P

HD = 64
V = pltpu.VMEM


def call(body, out, ins, scratch, cid, name, **kw):
    return pl.pallas_call(body, out_shape=out,
        in_specs=[pl.BlockSpec(memory_space=pltpu.VMEM)]*len(ins),
        out_specs=jax.tree.map(lambda _: pl.BlockSpec(memory_space=pltpu.VMEM), out),
        scratch_shapes=scratch, name=name,
        compiler_params=pltpu.CompilerParams(collective_id=cid, has_side_effects=True, vmem_limit_bytes=48<<20))(*ins)


def rc(src, dst, ss, rs, **dev):
    return pltpu.make_async_remote_copy(src_ref=src, dst_ref=dst, send_sem=ss, recv_sem=rs, device_id=dev, device_id_type=pl.DeviceIdType.MESH)


def greet(devs):
    b = pltpu.get_barrier_semaphore()
    for d in devs:
        pl.semaphore_signal(b, inc=1, device_id=d, device_id_type=pl.DeviceIdType.MESH)
    pl.semaphore_wait(b, len(devs))


def ag_line(x, cid, chunks=1):
    n = lax.axis_size("col"); zs = n//2
    T = x.shape[0]//chunks
    def body(x_ref, o_ref, su, sd, sm, ru, rd, rm, ls):
        me = lax.axis_index("col"); z = me//2; p = lax.rem(me,2); mate = me+1-2*p
        bar = pltpu.get_barrier_semaphore()
        def sig(d): pl.semaphore_signal(bar, inc=1, device_id={"col": d}, device_id_type=pl.DeviceIdType.MESH)
        lo = z > 0; hi = z < zs-1
        sig(mate)
        pl.when(lo)(lambda: sig(me-2)); pl.when(hi)(lambda: sig(me+2))
        pl.semaphore_wait(bar, 1 + lo.astype(jnp.int32) + hi.astype(jnp.int32))
        def part(ref, c): return ref.at[pl.ds(c*T, T)]
        def up(src, blk, c): return rc(part(src,c), part(o_ref.at[blk],c), su.at[blk//2,c], ru.at[blk//2,c], col=me+2)
        def dn(src, blk, c): return rc(part(src,c), part(o_ref.at[blk],c), sd.at[blk//2,c], rd.at[blk//2,c], col=me-2)
        def mt(src, blk, c): return rc(part(src,c), part(o_ref.at[blk],c), sm.at[blk//2,c], rm.at[blk//2,c], col=mate)
        for c in range(chunks):
            pl.when(hi)(lambda: up(x_ref, me, c).start())
            pl.when(lo)(lambda: dn(x_ref, me, c).start())
        for c in range(chunks):
            mt(x_ref, me, c).start()
        l = pltpu.make_async_copy(x_ref, o_ref.at[me], ls); l.start()
        for k in range(1, zs):
            for c in range(chunks):
                @pl.when(z-k >= 0)
                def _():
                    b = me-2*k
                    up(o_ref.at[b], b, c).wait_recv()
                    pl.when(hi)(lambda: up(o_ref.at[b], b, c).start())
                    mt(o_ref.at[b], b, c).start()
                @pl.when(z+k < zs)
                def _():
                    b = me+2*k
                    dn(o_ref.at[b], b, c).wait_recv()
                    pl.when(lo)(lambda: dn(o_ref.at[b], b, c).start())
                    mt(o_ref.at[b], b, c).start()
        l.wait()
        for j in range(zs):
            for c in range(chunks):
                b = 2*j+p
                mt(o_ref.at[b], b, c).wait_send()
                mt(o_ref.at[2*j+1-p], 2*j+1-p, c).wait_recv()
                @pl.when(hi & (j <= z))
                def _(): up(o_ref.at[b], b, c).wait_send()
                @pl.when(lo & (j >= z))
                def _(): dn(o_ref.at[b], b, c).wait_send()
    D=pltpu.SemaphoreType.DMA((zs,chunks))
    return call(body, jax.ShapeDtypeStruct((n,)+x.shape, x.dtype), [x], [D,D,D,D,D,D,pltpu.SemaphoreType.DMA], cid, "agline%d_%d"%(chunks,cid))


def rs_hier(parts, cid):
    n = lax.axis_size("col"); zs = n//2
    blk = parts.shape[1:]
    def body(x_ref, o_ref, buf1, stage, buf2, s1, r1, s2, r2):
        me = lax.axis_index("col"); z = me//2; p = lax.rem(me,2); mate = me+1-2*p
        far = [lax.rem(me+2*k, n) for k in range(zs)]
        matefar = [lax.rem(mate+2*k, n) for k in range(zs)]
        greet([{"col": mate}]+[{"col": d} for d in far[1:]])
        order = sorted(range(1,zs), key=lambda k: -min(k, zs-k)) + [0]
        cs=[]
        for k in order:
            c = rc(x_ref.at[matefar[k]], buf1.at[k], s1.at[k], r1.at[k], col=mate); c.start(); cs.append(c)
        for k in order:
            rc(x_ref.at[0], buf1.at[k], s1.at[k], r1.at[k], col=mate).wait_recv()
            tot = x_ref[far[k]].astype(jnp.float32) + buf1[k].astype(jnp.float32)
            if k:
                stage[k] = tot.astype(stage.dtype)
                c = rc(stage.at[k], buf2.at[zs-k], s2.at[k], r2.at[zs-k], col=far[k]); c.start(); cs.append(c)
        for k in order[::-1][1:]:
            rc(stage.at[0], buf2.at[k], s2.at[k], r2.at[k], col=mate).wait_recv()
            tot = tot + buf2[k].astype(jnp.float32)
        o_ref[...] = tot
        for c in cs: c.wait_send()
    D=pltpu.SemaphoreType.DMA
    return call(body, jax.ShapeDtypeStruct(blk, jnp.float32), [parts], [V((zs,)+blk, parts.dtype)]*3+[D((zs,)),D((zs,)),D((zs,)),D((zs,))], cid, "rshier%d"%cid)


def swap_groups(x, cid):
    count = lax.axis_size("row")
    secs = lax.axis_size("section")

    def body(x_ref, o_ref, ss, rs):
        s, r = lax.axis_index("section"), lax.axis_index("row")
        to = lax.rem(s + 1, secs)
        back = lax.rem(s + secs - 1, secs)
        b = pltpu.get_barrier_semaphore()
        for k in range(count):
            pl.semaphore_signal(
                b,
                inc=1,
                device_id={"section": back, "row": lax.rem(r + k, count)},
                device_id_type=pl.DeviceIdType.MESH,
            )
        pl.semaphore_wait(b, count)
        cs = []
        for k in range(count):
            d = lax.rem(r + k, count)
            c = rc(x_ref.at[d], o_ref.at[r], ss.at[k], rs.at[(count - k) % count], section=to, row=d)
            c.start()
            cs.append(c)
        for k in range(count):
            d = lax.rem(r + k, count)
            rc(x_ref.at[d], o_ref.at[d], ss.at[k], rs.at[k], section=to, row=d).wait_recv()
        for c in cs:
            c.wait_send()

    D = pltpu.SemaphoreType.DMA
    return call(
        body, jax.ShapeDtypeStruct(x.shape, x.dtype), [x], [D((count,)), D((count,))], cid, "swap"
    )


def stem_embed(first, conv, patch_weight, cid):
    imgs, height, width, ch = first.shape
    rows_n, cols_n = lax.axis_size("row"), lax.axis_size("col")
    n, zs = cols_n, cols_n // 2
    tall, deep_k = height + 2, patch_weight.shape[0]
    model = patch_weight.shape[1]
    group = width // 4
    tokens = imgs * (height // 4) * group
    f32, bf16 = jnp.float32, jnp.bfloat16
    steps = [(a, b) for a in (-1, 0, 1) for b in (-1, 0, 1) if (a, b) != (0, 0)]

    def body(
        x_ref, w_ref, p_ref, o_ref,
        row_in, col_f, col_out, col_in, cor_out, cor_in, side, shifted, deep, feat_f, feat, pieces,
        terms, near, stage, far_in,
        hs, hr, as_, ar, s1, r1, s2, r2,
    ):
        r, me = lax.axis_index("row"), lax.axis_index("col")
        z, par = me // 2, lax.rem(me, 2)
        mate = me + 1 - 2 * par
        bar = pltpu.get_barrier_semaphore()

        def there(a, b):
            ok = jnp.int32(1)
            if a == -1:
                ok = ok * (r > 0).astype(jnp.int32)
            if a == 1:
                ok = ok * (r < rows_n - 1).astype(jnp.int32)
            if b == -1:
                ok = ok * (me > 0).astype(jnp.int32)
            if b == 1:
                ok = ok * (me < cols_n - 1).astype(jnp.int32)
            return ok

        def signal(dev):
            pl.semaphore_signal(bar, inc=1, device_id=dev, device_id_type=pl.DeviceIdType.MESH)

        have = [there(a, b) for a, b in steps]
        total = jnp.int32(n - 1)
        for k in range(1, n):
            signal({"col": lax.rem(me + k, n)})
        for (a, b), ok in zip(steps, have):
            if a != 0:
                total = total + ok
                pl.when(ok == 1)(lambda: signal({"row": r + a, "col": me + b}))

        def edges(i, carry):
            v = x_ref[i].astype(f32)
            col_f[0, pl.ds(i, 1), :] = v[:1]
            col_f[1, pl.ds(i, 1), :] = v[width - 1 :]
            return carry

        lax.fori_loop(0, imgs * height, edges, 0, unroll=4)
        col_out[...] = col_f[...].astype(bf16)
        for e in range(2):
            for f in range(2):
                for i in range(imgs):
                    at = i * height + (height - 1) * e
                    side[0, i : i + 1, :] = col_f[f, at : at + 1, :]
                cor_out[2 * e + f] = side[0, :imgs, :].astype(bf16)

        def route(a, b):
            if b == 0:
                e = (a + 1) // 2
                img = x_ref.reshape(imgs, height, width, ch)
                return img.at[:, (height - 1) * e], row_in.at[1 - e], row_in.at[e]
            if a == 0:
                f = (b + 1) // 2
                return col_out.at[f], col_in.at[1 - f], col_in.at[f]
            e, f = (a + 1) // 2, (b + 1) // 2
            return cor_out.at[2 * e + f], cor_in.at[3 - 2 * e - f], cor_in.at[2 * e + f]

        pl.semaphore_wait(bar, total)
        for j, ((a, b), ok) in enumerate(zip(steps, have)):
            src, there_ref, here_ref = route(a, b)

            @pl.when(ok == 1)
            def _():
                rc(src, there_ref, hs.at[j], hr.at[7 - j], row=r + a, col=me + b).start()

            @pl.when(ok == 0)
            def _():
                here_ref[...] = jnp.zeros_like(here_ref)

        for j, ((a, b), ok) in enumerate(zip(steps, have)):
            src, there_ref, here_ref = route(a, b)

            @pl.when(ok == 1)
            def _():
                c = rc(src, here_ref, hs.at[j], hr.at[j], row=r + a, col=me + b)
                c.wait_recv()
                c.wait_send()

        for f in range(2):
            for i in range(imgs):
                base = i * tall
                side[f, base + 1 : base + 1 + height, :] = col_in[
                    f, i * height : (i + 1) * height, :
                ].astype(f32)
            for e in range(2):
                got = cor_in[2 * e + f].astype(f32)
                for i in range(imgs):
                    at = i * tall + (tall - 1) * e
                    side[f, at : at + 1, :] = got[i : i + 1]
        place = lax.broadcasted_iota(jnp.int32, (width, ch), 0)

        def put(at, v):
            v = v.astype(f32)
            left = jnp.broadcast_to(side[0, pl.ds(at, 1), :], (width, ch))
            right = jnp.broadcast_to(side[1, pl.ds(at, 1), :], (width, ch))
            shifted[0, at] = jnp.where(place == 0, left, pltpu.roll(v, 1, 0)).astype(bf16)
            shifted[1, at] = v.astype(bf16)
            shifted[2, at] = jnp.where(
                place == width - 1, right, pltpu.roll(v, width - 1, 0)
            ).astype(bf16)

        for i in range(imgs):
            put(i * tall, row_in[0, i])
            put(i * tall + tall - 1, row_in[1, i])

        for i in range(imgs):

            def fill(h, carry):
                put(i * tall + 1 + h, x_ref[i * height + h])
                return carry

            lax.fori_loop(0, height, fill, 0, unroll=4)

        part_k = deep_k // ch

        def image(i, carry):
            acc = x_ref[pl.ds(i * height, height)].reshape(height * width, ch).astype(f32)
            for a in range(3):
                for b in range(3):
                    win = shifted[b, pl.ds(i * tall + a, height)].reshape(height * width, ch)
                    acc = acc + jnp.dot(win, w_ref[a, b], preferred_element_type=f32)
            acc = jnp.maximum(acc, 0.0).astype(bf16).astype(f32)
            pixels = pl.multiple_of(i * height * width, height * width)
            for l in range(ch // 128):
                deep[l, pl.ds(pixels, height * width), :] = acc[:, 128 * l : 128 * (l + 1)]
            return carry

        lax.fori_loop(0, imgs, image, 0)
        for g in range(imgs * height // 4):
            for a in range(4):
                for b in range(4):
                    q = 4 * a + b
                    for l in range(ch // 128):
                        off = (q % part_k) * ch + 128 * l
                        feat_f[q // part_k, g * group : (g + 1) * group, off : off + 128] = deep[
                            l, pl.ds((4 * g + a) * width + b, group, stride=4), :
                        ]
        feat[...] = feat_f[...].astype(bf16)
        sent = []
        for k in range(1, n):
            d = lax.rem(me + k, n)
            c = rc(feat.at[d], pieces.at[me], as_.at[k], ar.at[n - k], col=d)
            c.start()
            sent.append(c)
        terms[me] = jnp.dot(feat[me], p_ref[...], preferred_element_type=f32).astype(bf16)
        for k in range(1, n):
            d = lax.rem(me + k, n)
            rc(feat.at[d], pieces.at[d], as_.at[k], ar.at[k], col=d).wait_recv()
            terms[d] = jnp.dot(pieces[d], p_ref[...], preferred_element_type=f32).astype(bf16)
        far = [lax.rem(me + 2 * k, n) for k in range(zs)]
        mate_far = [lax.rem(mate + 2 * k, n) for k in range(zs)]
        order = sorted(range(1, zs), key=lambda k: -min(k, zs - k)) + [0]
        for k in order:
            c = rc(terms.at[mate_far[k]], near.at[k], s1.at[k], r1.at[k], col=mate)
            c.start()
            sent.append(c)
        for k in order:
            rc(terms.at[0], near.at[k], s1.at[k], r1.at[k], col=mate).wait_recv()
            tot = terms[far[k]].astype(f32) + near[k].astype(f32)
            if k:
                stage[k] = tot.astype(bf16)
                c = rc(stage.at[k], far_in.at[zs - k], s2.at[k], r2.at[zs - k], col=far[k])
                c.start()
                sent.append(c)
        for k in order[::-1][1:]:
            rc(stage.at[0], far_in.at[k], s2.at[k], r2.at[k], col=mate).wait_recv()
            tot = tot + far_in[k].astype(f32)
        o_ref[...] = tot
        for c in sent:
            c.wait_send()

    D = pltpu.SemaphoreType.DMA
    pad = -(-imgs * tall // 8) * 8
    return call(
        body,
        jax.ShapeDtypeStruct((tokens, model), f32),
        [first.reshape(imgs * height, width, ch), conv, patch_weight],
        [
            V((2, imgs, width, ch), bf16),
            V((2, imgs * height, ch), f32),
            V((2, imgs * height, ch), bf16),
            V((2, imgs * height, ch), bf16),
            V((4, imgs, ch), bf16),
            V((4, imgs, ch), bf16),
            V((2, pad, ch), f32),
            V((3, imgs * tall, width, ch), bf16),
            V((ch // 128, imgs * height * width, 128), f32),
            V((n, tokens, deep_k), f32),
            V((n, tokens, deep_k), bf16),
            V((n, tokens, deep_k), bf16),
            V((n, tokens, model), bf16),
        ]
        + [V((zs, tokens, model), bf16)] * 3
        + [D((8,)), D((8,)), D((n,)), D((n,))]
        + [D((zs,))] * 4,
        cid,
        "stem",
    )


def layer_norm(vectors, gain_vec):
    row_mean = jnp.mean(vectors, axis=-1, keepdims=True)
    center = vectors - row_mean
    spread = jnp.mean(center * center, axis=-1, keepdims=True)
    return center * lax.rsqrt(spread + 1e-06) * gain_vec


def on_device(
    images,
    stem_first,
    stem_conv,
    patch_weight,
    position,
    gain_attn,
    w_qkv,
    w_out,
    gain_mlp,
    w_up,
    w_down,
):
    first_map = jnp.einsum(
        "ikhw,kc->ihwc", images[0], stem_first, preferred_element_type=jnp.float32
    )
    stem_maps = jnp.maximum(first_map, 0.0).astype(jnp.bfloat16)
    embedded = stem_embed(stem_maps, stem_conv, patch_weight, 0)
    n = lax.axis_size("col")
    rows_n = lax.axis_size("row")
    model_width = patch_weight.shape[1]
    img_count, cols_here, rows_here = images.shape[1], images.shape[4] // 4, images.shape[3] // 4
    local_tokens = (
        embedded.reshape(img_count, rows_here, cols_here, model_width).transpose(0, 2, 1, 3)
        + position.astype(jnp.float32)[None]
    ).astype(jnp.bfloat16)
    arrived = swap_groups(local_tokens.reshape(rows_n, -1, model_width), 3)
    tokens_in = (
        arrived.reshape(rows_n, img_count // rows_n, cols_here, rows_here, model_width)
        .transpose(1, 2, 0, 3, 4)
        .reshape(-1, model_width)
    )
    residual = tokens_in.astype(jnp.float32)
    normed = layer_norm(residual, gain_attn).astype(jnp.bfloat16)
    projected = jnp.einsum(
        "td,kdh->kth",
        ag_line(normed, 4, 4).reshape(-1, model_width),
        w_qkv,
        preferred_element_type=jnp.float32,
    ).astype(jnp.bfloat16)
    token_count = projected.shape[1]
    local_heads = w_out.shape[0] // HD
    split_heads = projected.reshape(3, token_count, local_heads, HD).transpose(0, 2, 1, 3)
    key_heads = split_heads[1]
    value_heads = split_heads[2]
    block_rows = math.gcd(token_count, 512)
    query_blocks = (
        split_heads[0]
        .reshape(local_heads, token_count // block_rows, block_rows, HD)
        .transpose(1, 0, 2, 3)
    )

    def attend(query_block):
        scores = jnp.einsum(
            "hqd,hkd->hqk", query_block, key_heads, preferred_element_type=jnp.float32
        ) * HD ** (-0.5)
        row_peak = jnp.max(scores, axis=-1, keepdims=True)
        expo = jnp.exp(scores - row_peak)
        prob_rows = (expo / jnp.sum(expo, axis=-1, keepdims=True)).astype(jnp.bfloat16)
        return jnp.einsum(
            "hqk,hkd->hqd", prob_rows, value_heads, preferred_element_type=jnp.float32
        ).astype(jnp.bfloat16)

    attended = lax.map(attend, query_blocks)
    mixed_heads = attended.transpose(0, 2, 1, 3).reshape(token_count, local_heads * HD)
    row_slice = mixed_heads
    after = residual + rs_hier(
        jnp.dot(row_slice, w_out, preferred_element_type=jnp.float32)
        .astype(jnp.bfloat16)
        .reshape(n, -1, model_width),
        5,
    )
    normed_mlp = layer_norm(after, gain_mlp).astype(jnp.bfloat16)
    hidden = jax.nn.gelu(
        jnp.dot(
            ag_line(normed_mlp, 6, 4).reshape(-1, model_width),
            w_up,
            preferred_element_type=jnp.float32,
        ),
        approximate=True,
    ).astype(jnp.bfloat16)
    row_slice = hidden
    encoded = (
        after
        + rs_hier(
        jnp.dot(row_slice, w_down, preferred_element_type=jnp.float32)
        .astype(jnp.bfloat16)
        .reshape(n, -1, model_width),
        7,
    )
    ).astype(jnp.bfloat16)
    return encoded.reshape(1, 1, cols_here, -1, model_width)


def solution(mesh):
    placed = (
        P("section", None, None, "row", "col"),
        P(),
        P(),
        P("col", None),
        P("col", "row", None),
        P(),
        P(None, None, "col"),
        P("col", None),
        P(),
        P(None, "col"),
        P("col", None),
    )
    return jax.shard_map(
        on_device,
        mesh=mesh,
        in_specs=placed,
        out_specs=P("section", "row", "col", None, None),
        check_vma=False,
    )
```

time: 134 us -> 113 us (0.84)
  other arithmetic: 12.2 us -> 2.78 us
  Pallas kernels: 105 us -> 99.4 us
  matrix products: 10.6 us -> 6.84 us
  local copies, waits for them, and re-layouts: 6.28 us -> 3.44 us
    convert_element_type x4 -> x3, other arithmetic: 6.94 us -> 1.18 us  [the longest x1 0.94 us: on_device(): position.astype(jnp.float32)[None]]
    pallas_call x8 -> x6, Pallas kernels: 105 us -> 99.4 us  [call(): pl.pallas_call(body, out_shape=out, in_specs=[pl.BlockSpec(memory_space=p...]
    concatenate x2 -> x0, other arithmetic: 3.69 us -> none  [the longest x1 2.91 us: halo(): jnp.concatenate([jnp.concatenate([got[a, b] for b in (-1, 0, 1)], axis=2)...]
    slice x7 -> x0, local copies, waits for them, and re-layouts: 3.6 us -> none  [the longest x1 3.5 us: stem_features(): padded[:, offset_a:offset_a + height, offset_b:offset_b + tile_width, :]]
    dot_general x11 -> x1, matrix products: 4.65 us -> 1.23 us  [on_device(): jnp.einsum('ikhw,kc->ihwc', images[0], stem_first, preferred_element_type...]
    unnamed x13 -> x15, local copies, waits for them, and re-layouts: 1.44 us -> 3.02 us
where the time goes in v2:
time: 113 us
  Pallas kernels  99.4 us (88%)
  matrix products  6.84 us (6%)
  local copies, waits for them, and re-layouts  3.44 us (3%)
  other arithmetic  2.78 us (2%)
    pallas_call x6, Pallas kernels, call(): pl.pallas_call(body, out_shape=out, in_specs=[pl.BlockSpec(memory_space=p...  99.4 us
    unnamed x15, local copies, waits for them, and re-layouts  3.02 us
    dot_general x1, matrix products, on_device(): jnp.dot(row_slice, w_down, preferred_element_type=jnp.float32)  2.6 us

profile of v2, /device:TPU:0, one launch (start us, length us, event | category | flops | bytes accessed | tf_op | source)
XLA Modules:
  0.0 112.7 jit_solution(5090568986067510398)
XLA Ops:
  0.0 0.9 convert_element_type.60
  0.9 1.2 %fusion.2 = bf16[2,16,32,256]{3,2,1,0:T(8,128)(2,1)S(1)} fusion(bf16[1,2,48,16,32]{2,4,3,1,0:T(8,128)(2,1)} %param.11, bf16[48,256]{1,0:T(8,128)(2,1)} %param.12), kind=kOutput, calls=%fused_computation.9 | convolution fusion | flops 25690112 | bytes 647168 | tf_op jit(solution)/shard_map/ikhw,kc->ihwc/dot_general | solution.py:380
  2.2 0.0 copy-start.1
  2.2 1.3 %copy-done.1 = bf16[3,3,256,256]{3,2,1,0:T(8,128)(2,1)S(1)} copy-done((bf16[3,3,256,256]{3,2,1,0:T(8,128)(2,1)S(1)}, bf16[3,3,256,256]{3,2,1,0:T(8,128)(2,1)}, u32[]{:S(2)}) %copy-start.1) | copy-done | bytes 1179672
  3.5 1.2 %copy-done.2 = bf16[512,1024]{1,0:T(8,128)(2,1)S(1)} copy-done((bf16[512,1024]{1,0:T(8,128)(2,1)S(1)}, bf16[512,1024]{1,0:T(8,128)(2,1)}, u32[]{:S(2)}) %copy-start.2) | copy-done | bytes 1048600
  4.7 35.5 %stem.1 = f32[64,1024]{1,0:T(8,128)S(1)} custom-call(bf16[32,32,256]{2,1,0:T(8,128)(2,1)S(1)} %bitcast.77, bf16[3,3,256,256]{3,2,1,0:T(8,128)(2,1)S(1)} %copy-done.1, bf16[512,1024]{1,0:T(8,128)(2,1)S(1)} %copy-done.2), custom_call_target="tpu_custom_call" | custom-call | tf_op jit(solution)/shard_map/stem/pallas_call | solution.py:16
  40.2 0.2 fusion.17
  40.4 0.0 copy-start.5
  40.4 6.0 %swap.1 = bf16[2,32,1024]{2,1,0:T(8,128)(2,1)S(1)} custom-call(bf16[2,32,1024]{2,1,0:T(8,128)(2,1)S(1)} %reshape.91.x_ref), custom_call_target="tpu_custom_call" | custom-call | tf_op jit(solution)/shard_map/swap/pallas_call | solution.py:16
  46.4 0.1 reshape.101
  46.5 0.1 fusion.36
  46.6 0.1 div.27
  46.7 0.2 multiply_reduce_fusion.2
  46.9 0.1 reshape.99
  47.1 0.1 rsqrt.20
  47.2 0.1 multiply_convert_fusion.1.x_ref
  47.3 0.2 copy-done.3
  47.5 0.3 copy.18
  47.8 14.2 %agline4_4.1 = bf16[8,64,1024]{2,1,0:T(8,128)(2,1)S(1)} custom-call(bf16[64,1024]{1,0:T(8,128)(2,1)S(1)} %multiply_convert_fusion.1.x_ref), custom_call_target="tpu_custom_call" | custom-call | tf_op jit(solution)/shard_map/agline4_4/pallas_call | solution.py:16
  62.0 0.6 fusion.41
  62.7 0.1 convert_element_type.68
  62.7 0.8 fusion.38
  63.6 1.1 convolution_convert_fusion.2
  64.7 0.4 convolution_convert_fusion
  65.2 14.1 %rshier5.1 = f32[64,1024]{1,0:T(8,128)S(1)} custom-call(bf16[8,64,1024]{2,1,0:T(8,128)(2,1)S(1)} %bitcast.75), custom_call_target="tpu_custom_call" | custom-call | tf_op jit(solution)/shard_map/rshier5/pallas_call | solution.py:16
  79.2 0.1 fusion.37
  79.4 0.2 multiply_reduce_fusion.1
  79.6 0.1 multiply_convert_fusion.x_ref
  79.7 15.6 %agline4_6.1 = bf16[8,64,1024]{2,1,0:T(8,128)(2,1)S(1)} custom-call(bf16[64,1024]{1,0:T(8,128)(2,1)S(1)} %multiply_convert_fusion.x_ref), custom_call_target="tpu_custom_call" | custom-call | tf_op jit(solution)/shard_map/agline4_6/pallas_call | solution.py:16
  95.3 2.6 %convolution_convert_fusion.1 = bf16[512,1024]{1,0:T(8,128)(2,1)S(1)} fusion(bf16[512,1024]{1,0:T(8,128)(2,1)S(1)} %copy-done, bf16[512,1024]{1,0:T(8,128)(2,1)S(1)} %bitcast.80, bf16[1024,512]{1,0:T(8,128)(2,1)} %param.20), kind=kOutput, calls=%fused_computation.7 | convolution fusion | flops 1076625408 | bytes 4194304 | tf_op jit(solution)/shard_map/dot_general | solution.py:452
  97.9 14.1 %rshier7.1 = f32[64,1024]{1,0:T(8,128)S(1)} custom-call(bf16[8,64,1024]{2,1,0:T(8,128)(2,1)S(1)} %bitcast.78), custom_call_target="tpu_custom_call" | custom-call | tf_op jit(solution)/shard_map/rshier7/pallas_call | solution.py:16
  112.0 0.7 fusion.21
  (15 shorter events, 0.1 us)
Async XLA Ops:
  0.0 95.3 %copy-start = (bf16[512,1024]{1,0:T(8,128)(2,1)S(1)}, bf16[512,1024]{1,0:T(8,128)(2,1)}, u32[]{:S(2)}) copy-start(bf16[512,1024]{1,0:T(8,128)(2,1)} %param.21) | copy-start | bytes 3145732
  2.2 1.3 %copy-start.1 = (bf16[3,3,256,256]{3,2,1,0:T(8,128)(2,1)S(1)}, bf16[3,3,256,256]{3,2,1,0:T(8,128)(2,1)}, u32[]{:S(2)}) copy-start(bf16[3,3,256,256]{3,2,1,0:T(8,128)(2,1)} %w_ref.1) | copy-start | bytes 3538948
  3.4 1.2 %copy-start.2 = (bf16[512,1024]{1,0:T(8,128)(2,1)S(1)}, bf16[512,1024]{1,0:T(8,128)(2,1)}, u32[]{:S(2)}) copy-start(bf16[512,1024]{1,0:T(8,128)(2,1)} %p_ref.1) | copy-start | bytes 3145732
  40.4 6.8 %copy-start.5 = (f32[1024]{0:T(1024)S(1)}, f32[1024]{0:T(1024)}, u32[]{:S(2)}) copy-start(f32[1024]{0:T(1024)} %param.16) | copy-start | bytes 12292
  46.4 1.1 %copy-start.3 = (bf16[3,1024,128]{2,1,0:T(8,128)(2,1)S(1)}, bf16[3,1024,128]{2,1,0:T(8,128)(2,1)}, u32[]{:S(2)}) copy-start(bf16[3,1024,128]{2,1,0:T(8,128)(2,1)} %param.17) | copy-start | bytes 2359300
  63.6 1.1 %copy-start.4 = (bf16[128,1024]{1,0:T(8,128)(2,1)S(1)}, bf16[128,1024]{1,0:T(8,128)(2,1)}, u32[]{:S(2)}) copy-start(bf16[128,1024]{1,0:T(8,128)(2,1)} %param.18) | copy-start | bytes 786436
  65.2 14.4 %copy-start.6 = (f32[1024]{0:T(1024)S(1)}, f32[1024]{0:T(1024)}, u32[]{:S(2)}) copy-start(f32[1024]{0:T(1024)} %param.19) | copy-start | bytes 12292

commit v3 on v2

v3 whole, which is shorter than its diff:
```python
import functools
import math

import jax
import jax.numpy as jnp
from jax import lax
from jax.experimental import pallas as pl
from jax.experimental.pallas import tpu as pltpu
from jax.sharding import PartitionSpec as P

HD = 64
V = pltpu.VMEM


def call(body, out, ins, scratch, cid, name, far=()):
    return pl.pallas_call(
        body,
        out_shape=out,
        in_specs=[
            pl.BlockSpec(memory_space=pl.ANY if i in far else pltpu.VMEM) for i in range(len(ins))
        ],
        out_specs=pl.BlockSpec(memory_space=pltpu.VMEM),
        scratch_shapes=scratch,
        name=name,
        compiler_params=pltpu.CompilerParams(
            collective_id=cid, has_side_effects=True, vmem_limit_bytes=56 << 20
        ),
    )(*ins)


def rc(src, dst, ss, rs, **dev):
    return pltpu.make_async_remote_copy(src_ref=src, dst_ref=dst, send_sem=ss, recv_sem=rs, device_id=dev, device_id_type=pl.DeviceIdType.MESH)


def stem_embed(first, conv, patch_weight, cid):
    imgs, height, width, ch = first.shape
    rows_n, cols_n = lax.axis_size("row"), lax.axis_size("col")
    n, zs = cols_n, cols_n // 2
    tall, deep_k = height + 2, patch_weight.shape[0]
    model = patch_weight.shape[1]
    group = width // 4
    tokens = imgs * (height // 4) * group
    f32, bf16 = jnp.float32, jnp.bfloat16
    steps = [(a, b) for a in (-1, 0, 1) for b in (-1, 0, 1) if (a, b) != (0, 0)]

    def body(
        x_ref, w_hbm, p_hbm, o_ref,
        row_in, col_f, col_out, col_in, cor_out, cor_in, side, shifted, deep, feat_f, feat, pieces,
        terms, near, stage, far_in,
        hs, hr, as_, ar, s1, r1, s2, r2,
        w_ref, p_ref, fetch,
    ):
        get_conv = pltpu.make_async_copy(w_hbm, w_ref, fetch.at[0])
        get_conv.start()
        get_patch = pltpu.make_async_copy(p_hbm, p_ref, fetch.at[1])
        get_patch.start()
        r, me = lax.axis_index("row"), lax.axis_index("col")
        z, par = me // 2, lax.rem(me, 2)
        mate = me + 1 - 2 * par
        bar = pltpu.get_barrier_semaphore()

        def there(a, b):
            ok = jnp.int32(1)
            if a == -1:
                ok = ok * (r > 0).astype(jnp.int32)
            if a == 1:
                ok = ok * (r < rows_n - 1).astype(jnp.int32)
            if b == -1:
                ok = ok * (me > 0).astype(jnp.int32)
            if b == 1:
                ok = ok * (me < cols_n - 1).astype(jnp.int32)
            return ok

        def signal(dev):
            pl.semaphore_signal(bar, inc=1, device_id=dev, device_id_type=pl.DeviceIdType.MESH)

        have = [there(a, b) for a, b in steps]
        total = jnp.int32(n - 1)
        for k in range(1, n):
            signal({"col": lax.rem(me + k, n)})
        for (a, b), ok in zip(steps, have):
            if a != 0:
                total = total + ok
                pl.when(ok == 1)(lambda: signal({"row": r + a, "col": me + b}))

        def edges(i, carry):
            v = x_ref[i].astype(f32)
            col_f[0, pl.ds(i, 1), :] = v[:1]
            col_f[1, pl.ds(i, 1), :] = v[width - 1 :]
            return carry

        lax.fori_loop(0, imgs * height, edges, 0, unroll=4)
        col_out[...] = col_f[...].astype(bf16)
        for e in range(2):
            for f in range(2):
                for i in range(imgs):
                    at = i * height + (height - 1) * e
                    side[0, i : i + 1, :] = col_f[f, at : at + 1, :]
                cor_out[2 * e + f] = side[0, :imgs, :].astype(bf16)

        def route(a, b):
            if b == 0:
                e = (a + 1) // 2
                img = x_ref.reshape(imgs, height, width, ch)
                return img.at[:, (height - 1) * e], row_in.at[1 - e], row_in.at[e]
            if a == 0:
                f = (b + 1) // 2
                return col_out.at[f], col_in.at[1 - f], col_in.at[f]
            e, f = (a + 1) // 2, (b + 1) // 2
            return cor_out.at[2 * e + f], cor_in.at[3 - 2 * e - f], cor_in.at[2 * e + f]

        pl.semaphore_wait(bar, total)
        for j, ((a, b), ok) in enumerate(zip(steps, have)):
            src, there_ref, here_ref = route(a, b)

            @pl.when(ok == 1)
            def _():
                rc(src, there_ref, hs.at[j], hr.at[7 - j], row=r + a, col=me + b).start()

            @pl.when(ok == 0)
            def _():
                here_ref[...] = jnp.zeros_like(here_ref)

        for j, ((a, b), ok) in enumerate(zip(steps, have)):
            src, there_ref, here_ref = route(a, b)

            @pl.when(ok == 1)
            def _():
                c = rc(src, here_ref, hs.at[j], hr.at[j], row=r + a, col=me + b)
                c.wait_recv()
                c.wait_send()

        for f in range(2):
            for i in range(imgs):
                base = i * tall
                side[f, base + 1 : base + 1 + height, :] = col_in[
                    f, i * height : (i + 1) * height, :
                ].astype(f32)
            for e in range(2):
                got = cor_in[2 * e + f].astype(f32)
                for i in range(imgs):
                    at = i * tall + (tall - 1) * e
                    side[f, at : at + 1, :] = got[i : i + 1]
        place = lax.broadcasted_iota(jnp.int32, (width, ch), 0)

        def put(at, v):
            v = v.astype(f32)
            left = jnp.broadcast_to(side[0, pl.ds(at, 1), :], (width, ch))
            right = jnp.broadcast_to(side[1, pl.ds(at, 1), :], (width, ch))
            shifted[0, at] = jnp.where(place == 0, left, pltpu.roll(v, 1, 0)).astype(bf16)
            shifted[1, at] = v.astype(bf16)
            shifted[2, at] = jnp.where(
                place == width - 1, right, pltpu.roll(v, width - 1, 0)
            ).astype(bf16)

        for i in range(imgs):
            put(i * tall, row_in[0, i])
            put(i * tall + tall - 1, row_in[1, i])

        for i in range(imgs):

            def fill(h, carry):
                put(i * tall + 1 + h, x_ref[i * height + h])
                return carry

            lax.fori_loop(0, height, fill, 0, unroll=4)

        part_k = deep_k // ch
        get_conv.wait()

        def image(i, carry):
            acc = x_ref[pl.ds(i * height, height)].reshape(height * width, ch).astype(f32)
            for a in range(3):
                for b in range(3):
                    win = shifted[b, pl.ds(i * tall + a, height)].reshape(height * width, ch)
                    acc = acc + jnp.dot(win, w_ref[a, b], preferred_element_type=f32)
            acc = jnp.maximum(acc, 0.0).astype(bf16).astype(f32)
            pixels = pl.multiple_of(i * height * width, height * width)
            for l in range(ch // 128):
                deep[l, pl.ds(pixels, height * width), :] = acc[:, 128 * l : 128 * (l + 1)]
            return carry

        lax.fori_loop(0, imgs, image, 0)
        for g in range(imgs * height // 4):
            for a in range(4):
                for b in range(4):
                    q = 4 * a + b
                    for l in range(ch // 128):
                        off = (q % part_k) * ch + 128 * l
                        feat_f[q // part_k, g * group : (g + 1) * group, off : off + 128] = deep[
                            l, pl.ds((4 * g + a) * width + b, group, stride=4), :
                        ]
        feat[...] = feat_f[...].astype(bf16)
        sent = []
        for k in range(1, n):
            d = lax.rem(me + k, n)
            c = rc(feat.at[d], pieces.at[me], as_.at[k], ar.at[n - k], col=d)
            c.start()
            sent.append(c)
        get_patch.wait()
        terms[me] = jnp.dot(feat[me], p_ref[...], preferred_element_type=f32).astype(bf16)
        for k in range(1, n):
            d = lax.rem(me + k, n)
            rc(feat.at[d], pieces.at[d], as_.at[k], ar.at[k], col=d).wait_recv()
            terms[d] = jnp.dot(pieces[d], p_ref[...], preferred_element_type=f32).astype(bf16)
        far = [lax.rem(me + 2 * k, n) for k in range(zs)]
        mate_far = [lax.rem(mate + 2 * k, n) for k in range(zs)]
        order = sorted(range(1, zs), key=lambda k: -min(k, zs - k)) + [0]
        for k in order:
            c = rc(terms.at[mate_far[k]], near.at[k], s1.at[k], r1.at[k], col=mate)
            c.start()
            sent.append(c)
        for k in order:
            rc(terms.at[0], near.at[k], s1.at[k], r1.at[k], col=mate).wait_recv()
            tot = terms[far[k]].astype(f32) + near[k].astype(f32)
            if k:
                stage[k] = tot.astype(bf16)
                c = rc(stage.at[k], far_in.at[zs - k], s2.at[k], r2.at[zs - k], col=far[k])
                c.start()
                sent.append(c)
        for k in order[::-1][1:]:
            rc(stage.at[0], far_in.at[k], s2.at[k], r2.at[k], col=mate).wait_recv()
            tot = tot + far_in[k].astype(f32)
        o_ref[...] = tot
        for c in sent:
            c.wait_send()

    D = pltpu.SemaphoreType.DMA
    pad = -(-imgs * tall // 8) * 8
    return call(
        body,
        jax.ShapeDtypeStruct((tokens, model), f32),
        [first.reshape(imgs * height, width, ch), conv, patch_weight],
        [
            V((2, imgs, width, ch), bf16),
            V((2, imgs * height, ch), f32),
            V((2, imgs * height, ch), bf16),
            V((2, imgs * height, ch), bf16),
            V((4, imgs, ch), bf16),
            V((4, imgs, ch), bf16),
            V((2, pad, ch), f32),
            V((3, imgs * tall, width, ch), bf16),
            V((ch // 128, imgs * height * width, 128), f32),
            V((n, tokens, deep_k), f32),
            V((n, tokens, deep_k), bf16),
            V((n, tokens, deep_k), bf16),
            V((n, tokens, model), bf16),
        ]
        + [V((zs, tokens, model), bf16)] * 3
        + [D((8,)), D((8,)), D((n,)), D((n,))]
        + [D((zs,))] * 4
        + [V(conv.shape, bf16), V(patch_weight.shape, bf16), D((2,))],
        cid,
        "stem",
        far=(1, 2),
    )


def layer_norm(vectors, gain_vec):
    row_mean = jnp.mean(vectors, axis=-1, keepdims=True)
    center = vectors - row_mean
    spread = jnp.mean(center * center, axis=-1, keepdims=True)
    return center * lax.rsqrt(spread + 1e-06) * gain_vec


def layer(x, gain_attn, w_qkv, w_out, gain_mlp, w_up, w_down, cid):
    n, rows_n, secs = lax.axis_size("col"), lax.axis_size("row"), lax.axis_size("section")
    zs = n // 2
    width = x.shape[2]
    mine = x.shape[0] * x.shape[1]
    tokens = n * mine
    inner, hidden = w_out.shape[0], w_down.shape[0]
    heads = inner // HD
    chunks = 4
    piece = mine // chunks
    f32, bf16 = jnp.float32, jnp.bfloat16
    q_rows = math.gcd(tokens, 256)

    def body(
        x_ref, g1_ref, g2_ref, wq_hbm, wo_hbm, wu_hbm, wd_hbm, o_ref,
        arrived, res, all1, all2, qkv, att, terms1, terms2,
        near1, stage1, far1, near2, stage2, far2,
        wq, wo, wu, wd, fetch,
        xs, xr, su1, sd1, sm1, ru1, rd1, rm1, su2, sd2, sm2, ru2, rd2, rm2,
        a1, b1, c1, d1, a2, b2, c2, d2,
    ):
        gets = []
        for j, (src, dst) in enumerate(((wq_hbm, wq), (wo_hbm, wo), (wu_hbm, wu), (wd_hbm, wd))):
            gets.append(pltpu.make_async_copy(src, dst, fetch.at[j]))
            gets[-1].start()
        sec, row, me = lax.axis_index("section"), lax.axis_index("row"), lax.axis_index("col")
        z, par = me // 2, lax.rem(me, 2)
        mate = me + 1 - 2 * par
        far = [lax.rem(me + 2 * k, n) for k in range(zs)]
        chips = [lax.rem(z + k, zs) for k in range(zs)]
        order = sorted(range(1, zs), key=lambda k: -min(k, zs - k)) + [0]
        to, back = lax.rem(sec + 1, secs), lax.rem(sec + secs - 1, secs)
        bar = pltpu.get_barrier_semaphore()

        def signal(dev):
            pl.semaphore_signal(bar, inc=1, device_id=dev, device_id_type=pl.DeviceIdType.MESH)

        signal({"col": mate})
        for k in range(1, zs):
            signal({"col": far[k]})
        for k in range(rows_n):
            signal({"section": back, "row": lax.rem(row + k, rows_n)})
        pl.semaphore_wait(bar, zs + rows_n)
        sent = []
        for k in range(rows_n):
            d = lax.rem(row + k, rows_n)
            c = rc(
                x_ref.at[d], arrived.at[row], xs.at[k], xr.at[(rows_n - k) % rows_n],
                section=to, row=d,
            )
            c.start()
            sent.append(c)
        for k in range(rows_n):
            d = lax.rem(row + k, rows_n)
            rc(x_ref.at[d], arrived.at[d], xs.at[k], xr.at[k], section=to, row=d).wait_recv()
        res[...] = arrived[...].reshape(mine, width).astype(f32)
        lo, hi = z > 0, z < zs - 1

        def gather(full, su, sd, sm, ru, rd, rm):
            def part(blk, c):
                return full.at[blk, pl.ds(c * piece, piece)]

            def up(blk, c):
                return rc(
                    part(blk, c), part(blk, c), su.at[blk // 2, c], ru.at[blk // 2, c], col=me + 2
                )

            def down(blk, c):
                return rc(
                    part(blk, c), part(blk, c), sd.at[blk // 2, c], rd.at[blk // 2, c], col=me - 2
                )

            def side(blk, c):
                return rc(
                    part(blk, c), part(blk, c), sm.at[blk // 2, c], rm.at[blk // 2, c], col=mate
                )

            for c in range(chunks):
                pl.when(hi)(lambda: up(me, c).start())
                pl.when(lo)(lambda: down(me, c).start())
            for c in range(chunks):
                side(me, c).start()
            for k in range(1, zs):
                for c in range(chunks):

                    @pl.when(z - k >= 0)
                    def _():
                        b = me - 2 * k
                        up(b, c).wait_recv()
                        pl.when(hi)(lambda: up(b, c).start())
                        side(b, c).start()

                    @pl.when(z + k < zs)
                    def _():
                        b = me + 2 * k
                        down(b, c).wait_recv()
                        pl.when(lo)(lambda: down(b, c).start())
                        side(b, c).start()

            for j in range(zs):
                for c in range(chunks):
                    b = 2 * j + par
                    side(b, c).wait_send()
                    side(2 * j + 1 - par, c).wait_recv()

                    @pl.when(hi & (j <= z))
                    def _():
                        up(b, c).wait_send()

                    @pl.when(lo & (j >= z))
                    def _():
                        down(b, c).wait_send()

        def scatter_sum(make, terms, near, stage, far_in, s1, r1, s2, r2):
            for k in order:
                chip = chips[k]
                terms[pl.ds(2 * chip, 2)] = make(chip).astype(bf16).reshape(2, mine, width)
                c = rc(
                    terms.at[2 * chip + 1 - par], near.at[k], s1.at[k], r1.at[k], col=mate
                )
                c.start()
                sent.append(c)
            for k in order:
                rc(terms.at[0], near.at[k], s1.at[k], r1.at[k], col=mate).wait_recv()
                tot = terms[far[k]].astype(f32) + near[k].astype(f32)
                if k:
                    stage[k] = tot.astype(bf16)
                    c = rc(stage.at[k], far_in.at[zs - k], s2.at[k], r2.at[zs - k], col=far[k])
                    c.start()
                    sent.append(c)
            for k in order[::-1][1:]:
                rc(stage.at[0], far_in.at[k], s2.at[k], r2.at[k], col=mate).wait_recv()
                tot = tot + far_in[k].astype(f32)
            return tot

        all1[me] = layer_norm(res[...], g1_ref[...]).astype(bf16)
        gather(all1, su1, sd1, sm1, ru1, rd1, rm1)
        gets[0].wait()
        every = all1[...].reshape(tokens, width)
        for j in range(3):
            qkv[j] = jnp.dot(every, wq[j], preferred_element_type=f32).astype(bf16)

        def attend(i, carry):
            at = pl.multiple_of(i * q_rows, q_rows)
            outs = []
            for h in range(heads):
                q = qkv[0, pl.ds(at, q_rows), h * HD : (h + 1) * HD]
                keys = qkv[1, :, h * HD : (h + 1) * HD]
                vals = qkv[2, :, h * HD : (h + 1) * HD]
                scores = lax.dot_general(
                    q, keys, (((1,), (1,)), ((), ())), preferred_element_type=f32
                ) * HD ** (-0.5)
                expo = jnp.exp(scores - jnp.max(scores, axis=-1, keepdims=True))
                probs = expo * (1.0 / jnp.sum(expo, axis=-1, keepdims=True))
                outs.append(jnp.dot(probs.astype(bf16), vals, preferred_element_type=f32))
            joined = outs[0] if heads == 1 else jnp.concatenate(outs, axis=-1)
            att[pl.ds(at, q_rows), :] = joined.astype(bf16)
            return carry

        lax.fori_loop(0, tokens // q_rows, attend, 0)
        gets[1].wait()

        def mixed(chip):
            rows = pl.ds(pl.multiple_of(chip * 2 * mine, 2 * mine), 2 * mine)
            return jnp.dot(att[rows, :], wo[...], preferred_element_type=f32)

        res[...] = res[...] + scatter_sum(mixed, terms1, near1, stage1, far1, a1, b1, c1, d1)
        all2[me] = layer_norm(res[...], g2_ref[...]).astype(bf16)
        gather(all2, su2, sd2, sm2, ru2, rd2, rm2)
        gets[2].wait()
        gets[3].wait()

        def mlp(chip):
            block = all2[pl.ds(2 * chip, 2)].reshape(2 * mine, width)
            mid = jax.nn.gelu(
                jnp.dot(block, wu[...], preferred_element_type=f32), approximate=True
            ).astype(bf16)
            return jnp.dot(mid, wd[...], preferred_element_type=f32)

        total = scatter_sum(mlp, terms2, near2, stage2, far2, a2, b2, c2, d2)
        o_ref[...] = (res[...] + total).astype(bf16)
        for c in sent:
            c.wait_send()

    D = pltpu.SemaphoreType.DMA
    blocks = V((n, mine, width), bf16)
    quarter = V((zs, mine, width), bf16)
    return call(
        body,
        jax.ShapeDtypeStruct((mine, width), bf16),
        [x, gain_attn.reshape(1, -1), gain_mlp.reshape(1, -1), w_qkv, w_out, w_up, w_down],
        [
            V(x.shape, bf16),
            V((mine, width), f32),
            blocks,
            blocks,
            V((3, tokens, inner), bf16),
            V((tokens, inner), bf16),
            blocks,
            blocks,
        ]
        + [quarter] * 6
        + [V(w_qkv.shape, bf16), V(w_out.shape, bf16), V(w_up.shape, bf16), V(w_down.shape, bf16)]
        + [D((4,)), D((rows_n,)), D((rows_n,))]
        + [D((zs, chunks))] * 12
        + [D((zs,))] * 8,
        cid,
        "layer",
        far=(3, 4, 5, 6),
    )


def on_device(
    images,
    stem_first,
    stem_conv,
    patch_weight,
    position,
    gain_attn,
    w_qkv,
    w_out,
    gain_mlp,
    w_up,
    w_down,
):
    first_map = jnp.einsum(
        "ikhw,kc->ihwc", images[0], stem_first, preferred_element_type=jnp.float32
    )
    stem_maps = jnp.maximum(first_map, 0.0).astype(jnp.bfloat16)
    embedded = stem_embed(stem_maps, stem_conv, patch_weight, 0)
    n = lax.axis_size("col")
    rows_n = lax.axis_size("row")
    model_width = patch_weight.shape[1]
    img_count, cols_here, rows_here = images.shape[1], images.shape[4] // 4, images.shape[3] // 4
    local_tokens = (
        embedded.reshape(img_count, rows_here, cols_here, model_width).transpose(0, 2, 1, 3)
        + position.astype(jnp.float32)[None]
    ).astype(jnp.bfloat16)
    encoded = layer(
        local_tokens.reshape(rows_n, -1, model_width),
        gain_attn,
        w_qkv,
        w_out,
        gain_mlp,
        w_up,
        w_down,
        1,
    )
    return (
        encoded.reshape(rows_n, img_count // rows_n, cols_here, rows_here, model_width)
        .transpose(1, 2, 0, 3, 4)
        .reshape(1, img_count // rows_n, cols_here, -1, model_width)
    )


def solution(mesh):
    placed = (
        P("section", None, None, "row", "col"),
        P(),
        P(),
        P("col", None),
        P("col", "row", None),
        P(),
        P(None, None, "col"),
        P("col", None),
        P(),
        P(None, "col"),
        P("col", None),
    )
    return jax.shard_map(
        on_device,
        mesh=mesh,
        in_specs=placed,
        out_specs=P("section", "row", "col", None, None),
        check_vma=False,
    )
```

time: 113 us -> 106 us (0.938)
  matrix products: 6.84 us -> 1.79 us
  other arithmetic: 2.78 us -> 1.16 us
    dot_general x3 -> x0, matrix products: 4.17 us -> none  [the longest x1 2.6 us: on_device(): jnp.dot(row_slice, w_down, preferred_element_type=jnp.float32)]
    reshape x1 -> x3, local copies, waits for them, and re-layouts: 0.04 us -> 2.34 us  [the longest x1 0.96 us: on_device(): encoded.reshape(rows_n, img_count // rows_n, cols_here, rows_here, model_...]
    unnamed x15 -> x4, local copies, waits for them, and re-layouts: 3.02 us -> 0.95 us
    pallas_call x6 -> x2, Pallas kernels: 99.4 us -> 99.4 us  [call(): pl.pallas_call(body, out_shape=out, in_specs=[pl.BlockSpec(memory_space=p...]
where the time goes in v3:
time: 106 us
  Pallas kernels  99.4 us (94%)
  local copies, waits for them, and re-layouts  3.34 us (3%)
  matrix products  1.79 us (2%)
  other arithmetic  1.16 us (1%)
    pallas_call x2, Pallas kernels, call(): pl.pallas_call(body, out_shape=out, in_specs=[pl.BlockSpec(memory_space=p...  99.4 us

profile of v3, /device:TPU:0, one launch (start us, length us, event | category | flops | bytes accessed | tf_op | source)
XLA Modules:
  0.0 105.8 jit_solution(17143947439070187613)
XLA Ops:
  0.0 0.0 copy-start
  0.0 0.9 copy-done
  1.0 1.8 %fusion = bf16[2,16,32,256]{3,2,1,0:T(8,128)(2,1)} fusion(bf16[1,2,48,16,32]{2,4,3,1,0:T(8,128)(2,1)S(1)} %copy-done, bf16[48,256]{1,0:T(8,128)(2,1)} %param.12), kind=kOutput, calls=%fused_computation.1 | convolution fusion | flops 25690112 | bytes 647168 | tf_op jit(solution)/shard_map/ikhw,kc->ihwc/dot_general | solution.py:491
  2.7 0.0 copy-start.1
  2.7 37.2 %stem.1 = f32[64,1024]{1,0:T(8,128)} custom-call(bf16[32,32,256]{2,1,0:T(8,128)(2,1)} %bitcast.17, bf16[3,3,256,256]{3,2,1,0:T(8,128)(2,1)} %w_hbm.1, bf16[512,1024]{1,0:T(8,128)(2,1)} %p_hbm.1), custom_call_target="tpu_custom_call" | custom-call | tf_op jit(solution)/shard_map/stem/pallas_call | solution.py:16
  40.0 0.0 copy-done.1
  40.0 1.1 %fusion.1 = bf16[2,8,4,1024]{3,2,1,0:T(4,128)(2,1)S(1)} fusion(f32[2,4,8,1024]{3,2,1,0:T(8,128)} %bitcast.18, f32[8,4,1024]{2,1,0:T(4,128)S(1)} %convert_element_type.10), kind=kLoop, calls=%fused_computation.3 | loop fusion | flops 131072 | bytes 524288 | tf_op jit(solution)/shard_map/convert_element_type | solution.py:503
  41.2 0.7 reshape.24.x_ref
  41.9 62.2 %layer.1 = bf16[64,1024]{1,0:T(8,128)(2,1)} custom-call(bf16[2,32,1024]{2,1,0:T(8,128)(2,1)} %reshape.24.x_ref, f32[1,1024]{1,0:T(1,128)} %bitcast.20, f32[1,1024]{1,0:T(1,128)} %bitcast.21, bf16[3,1024,128]{2,1,0:T(8,128)(2,1)} %wq_hbm.1, bf16[128,1024]{1,0:T(8,128)(2,1)} %wo_hbm.1, bf16[1024,512]{1,0:T(8,128)(2,1)} %wu_hbm.1, bf16[512,1024]{1,0:T(8,128)(2,1)} %wd_hbm.1), custom_call_target="tpu_custom_call" | custom-call | tf_op jit(solution)/shard_map/layer/pallas_call | solution.py:16
  104.0 1.0 reshape.27
  105.1 0.7 reshape.28
  (2 shorter events, 0.1 us)
Async XLA Ops:
  0.0 1.0 copy-start
  2.7 37.2 %copy-start.1 = (bf16[8,4,1024]{2,1,0:T(4,128)(2,1)S(1)}, bf16[8,4,1024]{2,1,0:T(4,128)(2,1)}, u32[]{:S(2)}) copy-start(bf16[8,4,1024]{2,1,0:T(4,128)(2,1)} %param.15) | copy-start | bytes 196612

commit v4 on v3

--- a/solution.py
+++ b/solution.py
@@ -40,6 +40,8 @@
     model = patch_weight.shape[1]
     group = width // 4
     tokens = imgs * (height // 4) * group
+    halves = 2 if imgs % 2 == 0 else 1
+    some = tokens // halves
     f32, bf16 = jnp.float32, jnp.bfloat16
     steps = [(a, b) for a in (-1, 0, 1) for b in (-1, 0, 1) if (a, b) != (0, 0)]
 
@@ -180,48 +182,88 @@
                 deep[l, pl.ds(pixels, height * width), :] = acc[:, 128 * l : 128 * (l + 1)]
             return carry
 
-        lax.fori_loop(0, imgs, image, 0)
-        for g in range(imgs * height // 4):
-            for a in range(4):
-                for b in range(4):
-                    q = 4 * a + b
-                    for l in range(ch // 128):
-                        off = (q % part_k) * ch + 128 * l
-                        feat_f[q // part_k, g * group : (g + 1) * group, off : off + 128] = deep[
-                            l, pl.ds((4 * g + a) * width + b, group, stride=4), :
-                        ]
-        feat[...] = feat_f[...].astype(bf16)
-        sent = []
-        for k in range(1, n):
-            d = lax.rem(me + k, n)
-            c = rc(feat.at[d], pieces.at[me], as_.at[k], ar.at[n - k], col=d)
-            c.start()
-            sent.append(c)
-        get_patch.wait()
-        terms[me] = jnp.dot(feat[me], p_ref[...], preferred_element_type=f32).astype(bf16)
-        for k in range(1, n):
-            d = lax.rem(me + k, n)
-            rc(feat.at[d], pieces.at[d], as_.at[k], ar.at[k], col=d).wait_recv()
-            terms[d] = jnp.dot(pieces[d], p_ref[...], preferred_element_type=f32).astype(bf16)
         far = [lax.rem(me + 2 * k, n) for k in range(zs)]
         mate_far = [lax.rem(mate + 2 * k, n) for k in range(zs)]
         order = sorted(range(1, zs), key=lambda k: -min(k, zs - k)) + [0]
-        for k in order:
-            c = rc(terms.at[mate_far[k]], near.at[k], s1.at[k], r1.at[k], col=mate)
-            c.start()
-            sent.append(c)
-        for k in order:
-            rc(terms.at[0], near.at[k], s1.at[k], r1.at[k], col=mate).wait_recv()
-            tot = terms[far[k]].astype(f32) + near[k].astype(f32)
-            if k:
-                stage[k] = tot.astype(bf16)
-                c = rc(stage.at[k], far_in.at[zs - k], s2.at[k], r2.at[zs - k], col=far[k])
+        reach = sorted(range(1, n), key=lambda k: -min(k, n - k))
+        sent = []
+        for half in range(halves):
+            lax.fori_loop(half * imgs // halves, (half + 1) * imgs // halves, image, 0)
+            bands = imgs * height // 4 // halves
+            for g in range(half * bands, (half + 1) * bands):
+                for a in range(4):
+                    for b in range(4):
+                        q = 4 * a + b
+                        for l in range(ch // 128):
+                            off = (q % part_k) * ch + 128 * l
+                            feat_f[q // part_k, g * group : (g + 1) * group, off : off + 128] = (
+                                deep[l, pl.ds((4 * g + a) * width + b, group, stride=4), :]
+                            )
+            rows = slice(half * some, (half + 1) * some)
+            feat[half] = feat_f[:, rows, :].astype(bf16)
+            for k in reach:
+                d = lax.rem(me + k, n)
+                c = rc(
+                    feat.at[half, d], pieces.at[half, me], as_.at[half, k], ar.at[half, n - k],
+                    col=d,
+                )
                 c.start()
                 sent.append(c)
-        for k in order[::-1][1:]:
-            rc(stage.at[0], far_in.at[k], s2.at[k], r2.at[k], col=mate).wait_recv()
-            tot = tot + far_in[k].astype(f32)
-        o_ref[...] = tot
+            pieces[half, me] = feat[half, me]
+        get_patch.wait()
+        for half in range(halves):
+            rows = slice(half * some, (half + 1) * some)
+
+            def combine(k):
+                rc(
+                    terms.at[half, 0], near.at[half, k], s1.at[half, k], r1.at[half, k], col=mate
+                ).wait_recv()
+                tot = terms[half, far[k]].astype(f32) + near[half, k].astype(f32)
+                if k:
+                    stage[half, k] = tot.astype(bf16)
+                    c = rc(
+                        stage.at[half, k], far_in.at[half, zs - k], s2.at[half, k],
+                        r2.at[half, zs - k], col=far[k],
+                    )
+                    c.start()
+                    sent.append(c)
+                else:
+                    o_ref[rows, :] = tot
+
+            for j, k in enumerate(order):
+                for d, off in ((far[k], 2 * k), (mate_far[k], None)):
+                    if off is None:
+                        off = lax.rem(d - me + n, n)
+                    if k or d is not far[k]:
+                        rc(
+                            feat.at[half, 0], pieces.at[half, d], as_.at[half, off],
+                            ar.at[half, off], col=d,
+                        ).wait_recv()
+                chip = lax.rem(z + k, zs)
+                both = pieces[half, pl.ds(2 * chip, 2)].reshape(2 * some, deep_k)
+                terms[half, pl.ds(2 * chip, 2)] = (
+                    jnp.dot(both, p_ref[...], preferred_element_type=f32)
+                    .astype(bf16)
+                    .reshape(2, some, model)
+                )
+                c = rc(
+                    terms.at[half, mate_far[k]], near.at[half, k], s1.at[half, k], r1.at[half, k],
+                    col=mate,
+                )
+                c.start()
+                sent.append(c)
+                if j:
+                    combine(order[j - 1])
+            combine(order[-1])
+        for half in range(halves):
+            rows = slice(half * some, (half + 1) * some)
+            tot = o_ref[rows, :]
+            for k in order[::-1][1:]:
+                rc(
+                    stage.at[half, 0], far_in.at[half, k], s2.at[half, k], r2.at[half, k], col=mate
+                ).wait_recv()
+                tot = tot + far_in[half, k].astype(f32)
+            o_ref[rows, :] = tot
         for c in sent:
             c.wait_send()
 
@@ -242,13 +284,13 @@
             V((3, imgs * tall, width, ch), bf16),
             V((ch // 128, imgs * height * width, 128), f32),
             V((n, tokens, deep_k), f32),
-            V((n, tokens, deep_k), bf16),
-            V((n, tokens, deep_k), bf16),
-            V((n, tokens, model), bf16),
+            V((halves, n, some, deep_k), bf16),
+            V((halves, n, some, deep_k), bf16),
+            V((halves, n, some, model), bf16),
         ]
-        + [V((zs, tokens, model), bf16)] * 3
-        + [D((8,)), D((8,)), D((n,)), D((n,))]
-        + [D((zs,))] * 4
+        + [V((halves, zs, some, model), bf16)] * 3
+        + [D((8,)), D((8,)), D((halves, n)), D((halves, n))]
+        + [D((halves, zs))] * 4
         + [V(conv.shape, bf16), V(patch_weight.shape, bf16), D((2,))],
         cid,
         "stem",
@@ -377,15 +419,7 @@
                         down(b, c).wait_send()
 
         def scatter_sum(make, terms, near, stage, far_in, s1, r1, s2, r2):
-            for k in order:
-                chip = chips[k]
-                terms[pl.ds(2 * chip, 2)] = make(chip).astype(bf16).reshape(2, mine, width)
-                c = rc(
-                    terms.at[2 * chip + 1 - par], near.at[k], s1.at[k], r1.at[k], col=mate
-                )
-                c.start()
-                sent.append(c)
-            for k in order:
+            def combine(k):
                 rc(terms.at[0], near.at[k], s1.at[k], r1.at[k], col=mate).wait_recv()
                 tot = terms[far[k]].astype(f32) + near[k].astype(f32)
                 if k:
@@ -393,6 +427,19 @@
                     c = rc(stage.at[k], far_in.at[zs - k], s2.at[k], r2.at[zs - k], col=far[k])
                     c.start()
                     sent.append(c)
+                return tot
+
+            for j, k in enumerate(order):
+                chip = chips[k]
+                terms[pl.ds(2 * chip, 2)] = make(chip).astype(bf16).reshape(2, mine, width)
+                c = rc(
+                    terms.at[2 * chip + 1 - par], near.at[k], s1.at[k], r1.at[k], col=mate
+                )
+                c.start()
+                sent.append(c)
+                if j:
+                    combine(order[j - 1])
+            tot = combine(order[-1])
             for k in order[::-1][1:]:
                 rc(stage.at[0], far_in.at[k], s2.at[k], r2.at[k], col=mate).wait_recv()
                 tot = tot + far_in[k].astype(f32)

time: 106 us -> 104 us (0.981)
  Pallas kernels: 99.4 us -> 97.3 us
    pallas_call x2, Pallas kernels: 99.4 us -> 97.3 us  [call(): pl.pallas_call(body, out_shape=out, in_specs=[pl.BlockSpec(memory_space=p...]
where the time goes in v4:
time: 104 us
  Pallas kernels  97.3 us (94%)
  local copies, waits for them, and re-layouts  3.34 us (3%)
  matrix products  1.79 us (2%)
  other arithmetic  1.16 us (1%)
    pallas_call x2, Pallas kernels, call(): pl.pallas_call(body, out_shape=out, in_specs=[pl.BlockSpec(memory_space=p...  97.3 us

profile of v4, /device:TPU:0, one launch (start us, length us, event | category | flops | bytes accessed | tf_op | source)
XLA Modules:
  0.0 103.7 jit_solution(10435318420918075311)
XLA Ops:
  0.0 0.0 copy-start
  0.0 0.9 copy-done
  1.0 1.8 %fusion = bf16[2,16,32,256]{3,2,1,0:T(8,128)(2,1)} fusion(bf16[1,2,48,16,32]{2,4,3,1,0:T(8,128)(2,1)S(1)} %copy-done, bf16[48,256]{1,0:T(8,128)(2,1)} %param.12), kind=kOutput, calls=%fused_computation.1 | convolution fusion | flops 25690112 | bytes 647168 | tf_op jit(solution)/shard_map/ikhw,kc->ihwc/dot_general | solution.py:538
  2.7 0.0 copy-start.1
  2.7 36.8 %stem.1 = f32[64,1024]{1,0:T(8,128)} custom-call(bf16[32,32,256]{2,1,0:T(8,128)(2,1)} %bitcast.17, bf16[3,3,256,256]{3,2,1,0:T(8,128)(2,1)} %w_hbm.1, bf16[512,1024]{1,0:T(8,128)(2,1)} %p_hbm.1), custom_call_target="tpu_custom_call" | custom-call | tf_op jit(solution)/shard_map/stem/pallas_call | solution.py:16
  39.5 0.0 copy-done.1
  39.6 1.1 %fusion.1 = bf16[2,8,4,1024]{3,2,1,0:T(4,128)(2,1)S(1)} fusion(f32[2,4,8,1024]{3,2,1,0:T(8,128)} %bitcast.18, f32[8,4,1024]{2,1,0:T(4,128)S(1)} %convert_element_type.10), kind=kLoop, calls=%fused_computation.3 | loop fusion | flops 131072 | bytes 524288 | tf_op jit(solution)/shard_map/convert_element_type | solution.py:550
  40.7 0.7 reshape.24.x_ref
  41.4 60.5 %layer.1 = bf16[64,1024]{1,0:T(8,128)(2,1)} custom-call(bf16[2,32,1024]{2,1,0:T(8,128)(2,1)} %reshape.24.x_ref, f32[1,1024]{1,0:T(1,128)} %bitcast.20, f32[1,1024]{1,0:T(1,128)} %bitcast.21, bf16[3,1024,128]{2,1,0:T(8,128)(2,1)} %wq_hbm.1, bf16[128,1024]{1,0:T(8,128)(2,1)} %wo_hbm.1, bf16[1024,512]{1,0:T(8,128)(2,1)} %wu_hbm.1, bf16[512,1024]{1,0:T(8,128)(2,1)} %wd_hbm.1), custom_call_target="tpu_custom_call" | custom-call | tf_op jit(solution)/shard_map/layer/pallas_call | solution.py:16
  101.9 1.0 reshape.27
  103.0 0.7 reshape.28
  (2 shorter events, 0.1 us)
Async XLA Ops:
  0.0 1.0 copy-start
  2.7 36.8 %copy-start.1 = (bf16[8,4,1024]{2,1,0:T(4,128)(2,1)S(1)}, bf16[8,4,1024]{2,1,0:T(4,128)(2,1)}, u32[]{:S(2)}) copy-start(bf16[8,4,1024]{2,1,0:T(4,128)(2,1)} %param.15) | copy-start | bytes 196612

commit v5 on v4

--- a/solution.py
+++ b/solution.py
@@ -32,7 +32,7 @@
     return pltpu.make_async_remote_copy(src_ref=src, dst_ref=dst, send_sem=ss, recv_sem=rs, device_id=dev, device_id_type=pl.DeviceIdType.MESH)
 
 
-def stem_embed(first, conv, patch_weight, cid):
+def stem_embed(first, conv, patch_weight, place_rows, cid):
     imgs, height, width, ch = first.shape
     rows_n, cols_n = lax.axis_size("row"), lax.axis_size("col")
     n, zs = cols_n, cols_n // 2
@@ -46,8 +46,8 @@
     steps = [(a, b) for a in (-1, 0, 1) for b in (-1, 0, 1) if (a, b) != (0, 0)]
 
     def body(
-        x_ref, w_hbm, p_hbm, o_ref,
-        row_in, col_f, col_out, col_in, cor_out, cor_in, side, shifted, deep, feat_f, feat, pieces,
+        x_ref, w_hbm, p_hbm, pos_ref, o_ref,
+        sums, row_in, col_f, col_out, col_in, cor_out, cor_in, side, shifted, deep, feat_f, feat, pieces,
         terms, near, stage, far_in,
         hs, hr, as_, ar, s1, r1, s2, r2,
         w_ref, p_ref, fetch,
@@ -228,7 +228,7 @@
                     c.start()
                     sent.append(c)
                 else:
-                    o_ref[rows, :] = tot
+                    sums[rows, :] = tot
 
             for j, k in enumerate(order):
                 for d, off in ((far[k], 2 * k), (mate_far[k], None)):
@@ -257,13 +257,17 @@
             combine(order[-1])
         for half in range(halves):
             rows = slice(half * some, (half + 1) * some)
-            tot = o_ref[rows, :]
+            tot = sums[rows, :]
             for k in order[::-1][1:]:
                 rc(
                     stage.at[half, 0], far_in.at[half, k], s2.at[half, k], r2.at[half, k], col=mate
                 ).wait_recv()
                 tot = tot + far_in[half, k].astype(f32)
-            o_ref[rows, :] = tot
+            step = pos_ref.shape[0]
+            for at in range(0, some, step):
+                o_ref[half * some + at : half * some + at + step, :] = (
+                    tot[at : at + step] + pos_ref[...].astype(f32)
+                ).astype(bf16)
         for c in sent:
             c.wait_send()
 
@@ -271,9 +275,10 @@
     pad = -(-imgs * tall // 8) * 8
     return call(
         body,
-        jax.ShapeDtypeStruct((tokens, model), f32),
-        [first.reshape(imgs * height, width, ch), conv, patch_weight],
+        jax.ShapeDtypeStruct((tokens, model), bf16),
+        [first.reshape(imgs * height, width, ch), conv, patch_weight, place_rows],
         [
+            V((tokens, model), f32),
             V((2, imgs, width, ch), bf16),
             V((2, imgs * height, ch), f32),
             V((2, imgs * height, ch), bf16),
@@ -305,7 +310,7 @@
     return center * lax.rsqrt(spread + 1e-06) * gain_vec
 
 
-def layer(x, gain_attn, w_qkv, w_out, gain_mlp, w_up, w_down, cid):
+def layer(x, gain_attn, w_qkv, w_out, gain_mlp, w_up, w_down, cols_here, per, cid):
     n, rows_n, secs = lax.axis_size("col"), lax.axis_size("row"), lax.axis_size("section")
     zs = n // 2
     width = x.shape[2]
@@ -317,6 +322,8 @@
     piece = mine // chunks
     f32, bf16 = jnp.float32, jnp.bfloat16
     q_rows = math.gcd(tokens, 256)
+    turned = per == 1 and cols_here % 8 == 0
+    out_shape = (cols_here, mine // cols_here, width) if turned else (mine, width)
 
     def body(
         x_ref, g1_ref, g2_ref, wq_hbm, wo_hbm, wu_hbm, wd_hbm, o_ref,
@@ -490,7 +497,10 @@
             return jnp.dot(mid, wd[...], preferred_element_type=f32)
 
         total = scatter_sum(mlp, terms2, near2, stage2, far2, a2, b2, c2, d2)
-        o_ref[...] = (res[...] + total).astype(bf16)
+        done = res[...] + total
+        if turned:
+            done = done.reshape(mine // cols_here, cols_here, width).transpose(1, 0, 2)
+        o_ref[...] = done.astype(bf16)
         for c in sent:
             c.wait_send()
 
@@ -499,7 +509,7 @@
     quarter = V((zs, mine, width), bf16)
     return call(
         body,
-        jax.ShapeDtypeStruct((mine, width), bf16),
+        jax.ShapeDtypeStruct(out_shape, bf16),
         [x, gain_attn.reshape(1, -1), gain_mlp.reshape(1, -1), w_qkv, w_out, w_up, w_down],
         [
             V(x.shape, bf16),
@@ -539,15 +549,12 @@
         "ikhw,kc->ihwc", images[0], stem_first, preferred_element_type=jnp.float32
     )
     stem_maps = jnp.maximum(first_map, 0.0).astype(jnp.bfloat16)
-    embedded = stem_embed(stem_maps, stem_conv, patch_weight, 0)
     n = lax.axis_size("col")
     rows_n = lax.axis_size("row")
     model_width = patch_weight.shape[1]
     img_count, cols_here, rows_here = images.shape[1], images.shape[4] // 4, images.shape[3] // 4
-    local_tokens = (
-        embedded.reshape(img_count, rows_here, cols_here, model_width).transpose(0, 2, 1, 3)
-        + position.astype(jnp.float32)[None]
-    ).astype(jnp.bfloat16)
+    place_rows = position.transpose(1, 0, 2).reshape(-1, model_width)
+    local_tokens = stem_embed(stem_maps, stem_conv, patch_weight, place_rows, 0)
     encoded = layer(
         local_tokens.reshape(rows_n, -1, model_width),
         gain_attn,
@@ -556,13 +563,16 @@
         gain_mlp,
         w_up,
         w_down,
+        cols_here,
+        img_count // rows_n,
         1,
     )
-    return (
-        encoded.reshape(rows_n, img_count // rows_n, cols_here, rows_here, model_width)
-        .transpose(1, 2, 0, 3, 4)
-        .reshape(1, img_count // rows_n, cols_here, -1, model_width)
-    )
+    per = img_count // rows_n
+    if encoded.ndim == 2:
+        encoded = encoded.reshape(rows_n, per, rows_here, cols_here, model_width).transpose(
+            1, 3, 0, 2, 4
+        )
+    return encoded.reshape(1, per, cols_here, -1, model_width)
 
 
 def solution(mesh):

time: 104 us -> 102 us (0.981)
  other arithmetic: 1.16 us -> 0 us
    reshape x3 -> x0, local copies, waits for them, and re-layouts: 2.34 us -> none  [the longest x1 0.96 us: on_device(): encoded.reshape(rows_n, img_count // rows_n, cols_here, rows_here, model_...]
    transpose x1, local copies, waits for them, and re-layouts: 0.05 us -> 1.53 us  [on_device(): place_rows = position.transpose(1, 0, 2).reshape(-1, model_width)]
    convert_element_type x2 -> x0, other arithmetic: 1.16 us -> none  [the longest x1 1.15 us: on_device(): local_tokens = (embedded.reshape(img_count, rows_here, cols_here, model_w...]
where the time goes in v5:
time: 102 us
  Pallas kernels  97.3 us (95%)
  local copies, waits for them, and re-layouts  3.11 us (3%)
  matrix products  1.8 us (2%)
    pallas_call x2, Pallas kernels, call(): pl.pallas_call(body, out_shape=out, in_specs=[pl.BlockSpec(memory_space=p...  97.3 us

profile of v5, /device:TPU:0, one launch (start us, length us, event | category | flops | bytes accessed | tf_op | source)
XLA Modules:
  0.0 102.2 jit_solution(12783072983146442548)
XLA Ops:
  0.0 0.0 copy-start
  0.0 1.5 %copy.15 = bf16[4,8,1024]{2,1,0:T(8,128)(2,1)} copy(bf16[4,8,1024]{2,0,1:T(4,128)(2,1)} %bitcast.21) | data formatting | bytes 131072 | tf_op jit(solution)/shard_map/transpose | solution.py:556
  1.5 0.0 copy-done
  1.5 1.8 %fusion = bf16[2,16,32,256]{3,2,1,0:T(8,128)(2,1)} fusion(bf16[1,2,48,16,32]{2,4,3,1,0:T(8,128)(2,1)S(1)} %copy-done, bf16[48,256]{1,0:T(8,128)(2,1)} %param.12), kind=kOutput, calls=%fused_computation.1 | convolution fusion | flops 25690112 | bytes 647168 | tf_op jit(solution)/shard_map/ikhw,kc->ihwc/dot_general | solution.py:548
  3.3 36.7 %stem.1 = bf16[64,1024]{1,0:T(8,128)(2,1)} custom-call(bf16[32,32,256]{2,1,0:T(8,128)(2,1)} %bitcast.17, bf16[3,3,256,256]{3,2,1,0:T(8,128)(2,1)} %w_hbm.1, bf16[512,1024]{1,0:T(8,128)(2,1)} %p_hbm.1, bf16[32,1024]{1,0:T(8,128)(2,1)} %bitcast.20), custom_call_target="tpu_custom_call" | custom-call | tf_op jit(solution)/shard_map/stem/pallas_call | solution.py:16
  40.1 60.6 %layer.1 = bf16[8,8,1024]{2,1,0:T(8,128)(2,1)} custom-call(bf16[2,32,1024]{2,1,0:T(8,128)(2,1)} %bitcast.18, f32[1,1024]{1,0:T(1,128)} %bitcast.22, f32[1,1024]{1,0:T(1,128)} %bitcast.23, bf16[3,1024,128]{2,1,0:T(8,128)(2,1)} %wq_hbm.1, bf16[128,1024]{1,0:T(8,128)(2,1)} %wo_hbm.1, bf16[1024,512]{1,0:T(8,128)(2,1)} %wu_hbm.1, bf16[512,1024]{1,0:T(8,128)(2,1)} %wd_hbm.1), custom_call_target="tpu_custom_call" | custom-call | tf_op jit(solution)/shard_map/layer/pallas_call | solution.py:16
  100.7 1.6 %copy.17 = bf16[1,1,8,8,1024]{4,3,2,1,0:T(8,128)(2,1)} copy(bf16[1,1,8,8,1024]{4,3,2,1,0:T(8,128)(2,1)} %bitcast.19) | data formatting | bytes 262144
Async XLA Ops:
  0.0 1.5 %copy-start = (bf16[1,2,48,16,32]{2,4,3,1,0:T(8,128)(2,1)S(1)}, bf16[1,2,48,16,32]{2,4,3,1,0:T(8,128)(2,1)}, u32[]{:S(2)}) copy-start(bf16[1,2,48,16,32]{2,4,3,1,0:T(8,128)(2,1)} %param.11) | copy-start | bytes 294916
